TPU v7x, 32 devices: a whole 2x2x4 slice. The times are simulated.
32 devices in a mesh: slab: 2 (over y), lat: 16 (over z, x, core).
Axes of the slice: x: 2, y: 2, z: 4, core: 2. Of those that a mesh axis runs over, the one named last changes fastest.
Arguments:
- coef: bfloat16 [384, 769, 256], P('lat', None, 'slab'), parts along dimension 2, may hold values from -0.375 to 0.375
- legendre: bfloat16 [384, 769, 360], P('lat'), may hold values from -0.21875 to 0.21875
- m_of_pair: int32 [384], replicated, may hold values from 0 to 383, each once
- row_of_slot: int32 [368], replicated, may hold values from -1 to 359, as said below
Outputs:
- grid_out: bfloat16 [368, 2, 128, 1440], P('lat', None, 'slab'), parts along dimension 2
- spectrum: float32 [768, 128], P('lat', 'slab'), parts along dimension 1
There are 2 independent parts, one for each index of `slab`. A program takes and returns all parts, laid end to end along the dimension named above; an argument that names none is the same for every part. Nothing has to cross between parts.
Inputs may be any that keep to these rules, and one draw needn't show every extreme that they name: `m_of_pair`: each of 0 to 383 appears once. `row_of_slot`: each northern row 0 to 359 is held by exactly one slot; all other slots hold -1.
All inputs are finite; a program needn't handle non-finite values.
Results may differ from a plain program's by a relative error of at most 0.0056.
Values may be sent and summed in bfloat16 or wider, within the bound.
No kernel may reach another device: no remote copies, remote signals or barrier semaphores. Data moves between devices by JAX's collectives and lax.ppermute only.
A program may use at most 192 MiB of HBM per device.

v0:
```python
import functools
import math

import jax
import jax.numpy as jnp
from jax import lax
from jax.experimental import pallas as pl
from jax.experimental.pallas import tpu as pltpu
from jax.sharding import PartitionSpec as P

NLON = 1440
GROUP = 8
LANES = 128


def legendre_kernel(low_ref, slot_ref, leg_ref, coef_ref, out_ref, pick_ref, leg32_ref, coef32_ref, rows_ref, *, length):
    group = pl.program_id(0)
    slots, heights = pick_ref.shape
    columns = coef_ref.shape[2]
    fields = columns // 2
    tiles = leg32_ref.shape[0]

    @pl.when(group == 0)
    def _():
        height = lax.broadcasted_iota(jnp.int32, (slots, heights), 1)
        pick_ref[...] = jnp.where(height == slot_ref[...], 1.0, 0.0).astype(jnp.bfloat16)

    for tile in range(tiles):
        start = tile * LANES
        width = min(LANES, heights - start)
        piece = leg_ref[:, :, start : start + width].astype(jnp.float32)
        leg32_ref[tile, :, :width] = piece.reshape(length * GROUP, width)
    coef32_ref[...] = coef_ref[...].astype(jnp.float32).reshape(coef32_ref.shape)
    position = lax.broadcasted_iota(jnp.int32, (1, length), 1)
    for member in range(GROUP):
        cut = length - 1 - low_ref[group * GROUP + member]
        pick_rows = pl.ds(member, length, stride=GROUP)
        leg = jnp.concatenate([leg32_ref[tile, pick_rows, :] for tile in range(tiles)], axis=1)
        leg = leg[:, :heights].astype(jnp.bfloat16)
        coef = jnp.transpose(coef32_ref[pick_rows, :])
        in_low = position < cut
        operand = []
        for segment in range(2):
            keep = in_low if segment == 0 else jnp.logical_not(in_low)
            parity = lax.rem(position if segment == 0 else position + cut, 2)
            north = jnp.where(keep, 1.0, 0.0)
            south = jnp.where(parity == 0, north, -north)
            for part in range(2):
                values = coef[part * fields : (part + 1) * fields]
                operand += [values * north, values * south]
        operand = jnp.concatenate(operand, axis=0).astype(jnp.bfloat16)
        fourier = jnp.dot(operand, leg, preferred_element_type=jnp.float32).astype(jnp.bfloat16)
        taken = lax.dot_general(
            pick_ref[...], fourier, (((1,), (1,)), ((), ())), preferred_element_type=jnp.float32
        )
        for kind in range(4):
            rows_ref[kind, pl.ds(member, slots, stride=GROUP), :] = taken[
                :, kind * columns : (kind + 1) * columns
            ]
    for kind in range(4):
        out_ref[:, kind] = rows_ref[kind].reshape(slots, GROUP, columns).astype(jnp.bfloat16)


def legendre_rows(low_m, row_of_slot, legendre, coef):
    length, pairs, heights = legendre.shape
    columns = coef.shape[2]
    slots = row_of_slot.shape[0]
    return pl.pallas_call(
        functools.partial(legendre_kernel, length=length),
        out_shape=jax.ShapeDtypeStruct((slots, 4, pairs, columns), jnp.bfloat16),
        grid_spec=pltpu.PrefetchScalarGridSpec(
            num_scalar_prefetch=1,
            grid=(pairs // GROUP,),
            in_specs=[
                pl.BlockSpec((slots, 1), lambda group, low: (0, 0)),
                pl.BlockSpec((length, GROUP, heights), lambda group, low: (0, group, 0)),
                pl.BlockSpec((length, GROUP, columns), lambda group, low: (0, group, 0)),
            ],
            out_specs=pl.BlockSpec((slots, 4, GROUP, columns), lambda group, low: (0, 0, group, 0)),
            scratch_shapes=[
                pltpu.VMEM((slots, heights), jnp.bfloat16),
                pltpu.VMEM((pl.cdiv(heights, LANES), length * GROUP, LANES), jnp.float32),
                pltpu.VMEM((length * GROUP, columns), jnp.float32),
                pltpu.VMEM((4, slots * GROUP, columns), jnp.float32),
            ],
        ),
        compiler_params=pltpu.CompilerParams(vmem_limit_bytes=56 << 20),
        cost_estimate=pl.CostEstimate(
            flops=2 * pairs * 4 * columns * heights * (length + slots),
            bytes_accessed=2 * (legendre.size + coef.size + slots * 4 * pairs * columns),
            transcendentals=0,
        ),
    )(low_m, row_of_slot[:, None], legendre, coef)


def legendre_rows_plain(low_m, row_of_slot, legendre, coef):
    length = legendre.shape[0]
    fields = coef.shape[2] // 2
    position = jnp.arange(length, dtype=jnp.int32)[:, None]
    cut = (length - 1 - low_m)[None, :]
    in_low = position < cut
    parity = jnp.where(in_low, position, position + cut) % 2
    sign = jnp.where(parity == 0, 1.0, -1.0).astype(jnp.bfloat16)[:, :, None]
    kinds = []
    for keep in (in_low, ~in_low):
        kept = jnp.where(keep[:, :, None], coef, jnp.zeros((), coef.dtype))
        for part in range(2):
            values = kept[:, :, part * fields : (part + 1) * fields]
            kinds.append(jnp.concatenate([values, values * sign], axis=2))
    fourier = jnp.einsum(
        "kph,kpqc->hqpc", legendre, jnp.stack(kinds, axis=2), preferred_element_type=jnp.float32
    ).astype(jnp.bfloat16)
    taken = jnp.take(fourier, jnp.maximum(row_of_slot, 0), axis=0)
    return jnp.where((row_of_slot >= 0)[:, None, None, None], taken, jnp.zeros((), taken.dtype))


def dft_kernel(rows_ref, table_ref, out_ref):
    for slot in range(out_ref.shape[0]):
        rows = rows_ref[:, slot].reshape(table_ref.shape[0], rows_ref.shape[3])
        values = lax.dot_general(
            rows, table_ref[...], (((0,), (0,)), ((), ())), preferred_element_type=jnp.float32
        )
        out_ref[slot] = values.astype(jnp.bfloat16).reshape(out_ref.shape[1:])


def dft_rows(rows, table, step=2):
    sources, slots, depth, columns = rows.shape
    out_block = (step, 2, columns // 2, table.shape[1])
    return pl.pallas_call(
        dft_kernel,
        out_shape=jax.ShapeDtypeStruct((slots,) + out_block[1:], jnp.bfloat16),
        grid=(pl.cdiv(slots, step),),
        in_specs=[
            pl.BlockSpec((sources, step, depth, columns), lambda block: (0, block, 0, 0)),
            pl.BlockSpec(table.shape, lambda block: (0, 0), pipeline_mode=pl.Buffered(1)),
        ],
        out_specs=pl.BlockSpec(out_block, lambda block: (block, 0, 0, 0)),
        compiler_params=pltpu.CompilerParams(vmem_limit_bytes=40 << 20),
        cost_estimate=pl.CostEstimate(
            flops=2 * slots * columns * table.size,
            bytes_accessed=2 * (rows.size + table.size + slots * columns * table.shape[1]),
            transcendentals=0,
        ),
    )(rows, table)


def dft_rows_plain(rows, table):
    sources, slots, depth, columns = rows.shape
    values = jnp.einsum(
        "dlkc,dkj->lcj", rows, table.reshape(sources, depth, -1), preferred_element_type=jnp.float32
    )
    return values.astype(jnp.bfloat16).reshape(slots, 2, columns // 2, -1)


def dft_table(m_of_pair, wave_count, pairs_dev):
    low = m_of_pair.reshape(-1, 1, pairs_dev)
    wave = jnp.concatenate([low, wave_count - 1 - low], axis=1)[..., None]
    longitude = jnp.arange(NLON, dtype=jnp.int32)
    angles = (wave * longitude % NLON).astype(jnp.float32) * (2.0 * math.pi / NLON)
    weights = jnp.where(wave == 0, 1.0, 2.0).astype(jnp.float32)
    table = jnp.stack([weights * jnp.cos(angles), -weights * jnp.sin(angles)], axis=2)
    return table.astype(jnp.bfloat16).reshape(-1, NLON)


def spectrum_terms(coef, low_m):
    pairs_dev, length, columns = coef.shape
    wave_count = length - 1
    fields = columns // 2
    squares = coef.astype(jnp.float32) ** 2
    power_sum = squares[:, :, :fields] + squares[:, :, fields:]
    padded = jnp.concatenate(
        [jnp.zeros((pairs_dev, wave_count, fields), jnp.float32), power_sum[:, :wave_count]], axis=1
    )
    shifted = jax.vmap(
        lambda values, offset: lax.dynamic_slice_in_dim(values, offset, wave_count, 0)
    )(padded, wave_count - low_m)
    degree = jnp.arange(wave_count, dtype=jnp.int32)
    high_keep = (degree[None, :] >= (wave_count - 1 - low_m)[:, None]).astype(jnp.float32)
    high_terms = power_sum[:, 1:] * high_keep[:, :, None]
    low_weight = jnp.where(low_m == 0, 1.0, 2.0).astype(jnp.float32)
    return jnp.sum(low_weight[:, None, None] * shifted + 2.0 * high_terms, axis=0)


def local(coef, legendre, m_of_pair, row_of_slot):
    pairs_dev, length, columns = coef.shape
    wave_count = length - 1
    device = lax.axis_index("lat")
    low_m = lax.dynamic_slice_in_dim(m_of_pair, device * pairs_dev, pairs_dev)
    aligned = pairs_dev % GROUP == 0 and (4 * pairs_dev) % 16 == 0
    head = legendre_rows if aligned else legendre_rows_plain
    outgoing = head(
        low_m, row_of_slot, jnp.transpose(legendre, (1, 0, 2)), jnp.transpose(coef, (1, 0, 2))
    )
    outgoing = outgoing.reshape(outgoing.shape[0], 4 * pairs_dev, columns)
    incoming = lax.all_to_all(outgoing, "lat", split_axis=0, concat_axis=0, tiled=True)
    sources = m_of_pair.shape[0] // pairs_dev
    shaped = incoming.reshape(sources, -1, 4 * pairs_dev, columns)
    table = dft_table(m_of_pair, wave_count, pairs_dev)
    grid_out = (dft_rows if aligned else dft_rows_plain)(shaped, table)
    summed = lax.psum_scatter(spectrum_terms(coef, low_m), "lat", scatter_dimension=0, tiled=True)
    local_degree = (
        device * summed.shape[0] + jnp.arange(summed.shape[0], dtype=jnp.int32)
    ).astype(jnp.float32)
    spectrum = summed * (wave_count / (2.0 * local_degree + 1.0))[:, None]
    return (grid_out, spectrum)


def solution(mesh):
    in_specs = (P("lat", None, "slab"), P("lat", None, None), P(), P())
    out_specs = (P("lat", None, "slab", None), P("lat", "slab"))
    return jax.shard_map(local, mesh=mesh, in_specs=in_specs, out_specs=out_specs, check_vma=False)
```

profile of v0, /device:TPU:15, one launch (start us, length us, event | category | flops | bytes accessed | tf_op | source)
XLA Modules:
  0.0 276.2 jit_solution(12299667509548145381)
XLA Ops:
  7.2 1.5 broadcast_in_dim.36.slot_ref
  8.6 1.3 compare_select_fusion.2
  9.9 32.3 %shard_map.59 = bf16[368,4,24,128]{3,2,1,0:T(8,128)(2,1)} custom-call(s32[24]{0:T(128)} %get-tuple-element.3.low_ref, s32[368,1]{1,0:T(8,128)} %broadcast_in_dim.36.slot_ref, bf16[769,24,360]{2,1,0:T(8,128)(2,1)} %bitcast.14, bf16[769,24,128]{2,1,0:T(8,128)(2,1)} %bitcast.13), custom_call_target="tpu_custom_call" | custom-call | flops 10059448320 | bytes 27057024 | tf_op jit(solution)/shard_map/pallas_call | solution.py:68
  42.2 6.6 %all-to-all-start = ((bf16[368,96,128]{2,1,0:T(8,128)(2,1)}), bf16[368,96,128]{2,1,0:T(8,128)(2,1)}, u32[]{:S(2)}, u32[]{:S(2)}) async-start(bf16[368,96,128]{2,1,0:T(8,128)(2,1)} %bitcast.12), calls=%async_computation | async-start | bytes 18087936 | tf_op jit(solution)/shard_map/all_to_all | solution.py:195
  48.7 0.0 reduce-scatter.2.cloned.1.call-start
  48.8 6.6 %convert_multiply_fusion = f32[24,769,128]{2,0,1:T(8,128)} fusion(bf16[24,769,128]{2,0,1:T(8,128)(2,1)} %param.4), kind=kLoop, calls=%fused_computation.2 | loop fusion | flops 4724736 | bytes 14174208 | tf_op jit(solution)/shard_map/integer_pow | solution.py:169
  55.4 12.7 %slice_add_fusion = f32[24,769,64]{2,0,1:T(8,128)} fusion(f32[24,769,128]{2,0,1:T(8,128)} %convert_multiply_fusion), kind=kLoop, calls=%fused_computation.1 | loop fusion | flops 1181184 | bytes 14174208 | tf_op jit(solution)/shard_map/add | solution.py:170
  68.1 0.0 slice-start
  68.1 3.7 %slice-done = f32[24,768,64]{2,0,1:T(8,128)S(1)} async-done(((f32[24,769,64]{2,0,1:T(8,128)}), f32[24,768,64]{2,0,1:T(8,128)S(1)}, s32[]{:S(2)}) %slice-start) | async-done | bytes 4718616 | tf_op jit(solution)/shard_map/slice | solution.py:172
  71.8 8.2 %concatenate.20 = f32[24,1536,64]{2,0,1:T(8,128)} pad(f32[24,768,64]{2,0,1:T(8,128)S(1)} %slice-done, f32[]{:T(128)} %constant.23.clone.1), padding=0_0x768_0x0_0 | pad | bytes 14155780 | tf_op jit(solution)/shard_map/concatenate | solution.py:171
  80.1 0.0 copy-done.2
  80.1 23.8 %gather_fusion = f32[24,768,64]{2,0,1:T(8,128)} fusion(f32[24,1536,64]{2,0,1:T(8,128)} %concatenate.20, s32[24]{0:T(128)S(1)} %fusion.10), kind=kCustom, calls=%fused_computation | custom fusion | bytes 9437472 | tf_op jit(solution)/shard_map/vmap()/gather | solution.py:175
  103.9 0.0 copy-start.1
  103.9 9.2 %fusion.2 = f32[768,64]{1,0:T(8,128)} fusion(f32[24,769,64]{2,0,1:T(8,128)} %slice_add_fusion, f32[24,768,64]{2,0,1:T(8,128)} %gather_fusion, f32[24,768]{0,1:T(8,128)S(1)} %fusion.8, f32[24]{0:T(128)S(1)} %get-tuple-element.2), kind=kLoop, calls=%fused_computation.6 | loop fusion | flops 5849088 | bytes 9707616 | tf_op jit(solution)/shard_map/reduce_sum | solution.py:181
  113.2 0.0 reduce-scatter.2.cloned.1.call-update
  113.2 0.0 copy-done.1
  113.2 0.1 concatenate.18
  113.4 21.3 %multiply_convert_fusion.1 = (bf16[16,2,1,24,1440]{4,3,2,1,0:T(8,128)(2,1)S(1)}, bf16[16,2,1,24,1440]{4,3,2,1,0:T(8,128)(2,1)S(1)}) fusion(s32[16,2,24]{2,1,0:T(2,128)S(1)} %pad_add_fusion, f32[16,2,24]{2,1,0:T(2,128)S(1)} %get-tuple-element.6, f32[16,2,24]{2,1,0:T(2,128)S(1)} %get-tuple-element.7), kind=kLoop, calls=%fused_computation.12 | loop fusion | flops 14376960 | bytes 4432896 | tf_op jit(solution)/shard_map/convert
  134.7 2.6 pad_maximum_fusion
  137.3 78.8 %reduce-scatter.2.cloned.1.call-done = f32[48,64]{1,0:T(8,128)} async-done(((f32[768,64]{1,0:T(8,128)}), f32[48,64]{1,0:T(8,128)}) %reduce-scatter.2.cloned.1.call-update) | async-done | bytes 12304 | tf_op jit(solution)/shard_map/reduce_scatter | solution.py:200
  216.1 1.4 broadcast_multiply_fusion
  217.5 30.2 %all-to-all-done = bf16[368,96,128]{2,1,0:T(8,128)(2,1)} async-done(((bf16[368,96,128]{2,1,0:T(8,128)(2,1)}), bf16[368,96,128]{2,1,0:T(8,128)(2,1)}, u32[]{:S(2)}, u32[]{:S(2)}) %all-to-all-start) | async-done | bytes 9044000 | tf_op jit(solution)/shard_map/all_to_all | solution.py:195
  247.7 2.3 copy-done
  250.1 19.3 %shard_map.60 = bf16[23,2,64,1440]{3,2,1,0:T(8,128)(2,1)} custom-call(bf16[16,23,96,128]{3,2,1,0:T(8,128)(2,1)} %bitcast.3.rows_ref, bf16[1536,1440]{1,0:T(8,128)(2,1)S(1)} %bitcast.11), custom_call_target="tpu_custom_call" | custom-call | flops 13023313920 | bytes 21946368 | tf_op jit(solution)/shard_map/pallas_call | solution.py:129
  (9 shorter events, 0.1 us)
Async XLA Ops:
  42.2 205.5 %all-to-all-start = ((bf16[368,96,128]{2,1,0:T(8,128)(2,1)}), bf16[368,96,128]{2,1,0:T(8,128)(2,1)}, u32[]{:S(2)}, u32[]{:S(2)}) async-start(bf16[368,96,128]{2,1,0:T(8,128)(2,1)} %bitcast.12), calls=%async_computation | async-start | bytes 18087936 | tf_op jit(solution)/shard_map/all_to_all | solution.py:195
  48.7 167.3 %reduce-scatter.2.cloned.1.call-start = ((), (), s32[]{:S(2)}) async-start(), calls=%async_computation.2 | async-start | bytes 417792 | tf_op jit(solution)/shard_map/reduce_scatter | solution.py:200
  68.1 3.7 %slice-start = ((f32[24,769,64]{2,0,1:T(8,128)}), f32[24,768,64]{2,0,1:T(8,128)S(1)}, s32[]{:S(2)}) async-start(f32[24,769,64]{2,0,1:T(8,128)} %slice_add_fusion), calls=%async_computation.3 | async-start | bytes 18874368 | tf_op jit(solution)/shard_map/slice | solution.py:172
  71.8 8.2 %copy-start.2 = (s32[24]{0:T(128)S(1)}, s32[24]{0:T(128)}, u32[]{:S(2)}) copy-start(s32[24]{0:T(128)} %get-tuple-element.3.low_ref) | copy-start | bytes 292
  103.9 9.3 %copy-start.1 = (s32[384]{0:T(512)S(1)}, s32[384]{0:T(512)}, u32[]{:S(2)}) copy-start(s32[384]{0:T(512)} %param.6) | copy-start | bytes 4612
  247.7 2.3 copy-start
Sparse Core Ops, SparseCore 0:
  113.3 102.7 reduce-scatter.1
where the time goes:
time: 277 us; the launch traced here: 276 us
  waiting for transfers between devices  109 us (39%)
  other arithmetic  55.3 us (20%)
  Pallas kernels  51.6 us (19%)
  local copies, waits for them, and re-layouts  39.6 us (14%)
  between operations  14.1 us (5%)
  starting transfers between devices  6.59 us (2%)
    reduce_scatter x1, waiting for transfers between devices, local(): lax.psum_scatter(spectrum_terms(coef, low_m), 'lat', scatter_dimension=0,...  78.8 us
    pallas_call x1, Pallas kernels, legendre_rows(): pl.pallas_call(functools.partial(legendre_kernel, length=length), out_sha...  32.3 us
    all_to_all x1, waiting for transfers between devices, local(): lax.all_to_all(outgoing, 'lat', split_axis=0, concat_axis=0, tiled=True)  30.2 us
    gather x1, local copies, waits for them, and re-layouts, spectrum_terms(): lax.dynamic_slice_in_dim(values, offset, wave_count, 0)  23.8 us
    another operation x1, other arithmetic  21.3 us
    pallas_call x1, Pallas kernels, dft_rows(): pl.pallas_call(dft_kernel, out_shape=jax.ShapeDtypeStruct((slots,) + out_...  19.3 us
    add x1, other arithmetic, spectrum_terms(): power_sum = squares[:, :, :fields] + squares[:, :, fields:]  12.7 us
    reduce_sum x1, other arithmetic, spectrum_terms(): jnp.sum(low_weight[:, None, None] * shifted + 2.0 * high_terms, axis=0)  9.24 us
  transfers between devices with their start and end apart: 2, of which 2 were waited for; matrix products, arithmetic and copies ran while one was open for 31% of the time, Pallas kernels for 0%

commit v1 on v0

v1 whole, which is shorter than its diff:
```python
import functools
import math

import jax
import jax.numpy as jnp
from jax import lax
from jax.experimental import pallas as pl
from jax.experimental.pallas import tpu as pltpu
from jax.sharding import PartitionSpec as P

NLON = 1440
GROUP = 8
LANES = 128


def legendre_kernel(
    wave_ref, slot_ref, leg_ref, coef_ref, out_ref, pick_ref, leg32_ref, coef32_ref, rows_ref, *, length, first, pairs_dev, unroll
):
    group = pl.program_id(0)
    base = lax.axis_index("lat") * pairs_dev + (first + group) * GROUP
    slots, heights = pick_ref.shape
    columns = coef_ref.shape[2]
    fields = columns // 2
    tiles = leg32_ref.shape[0]

    @pl.when(group == 0)
    def _():
        height = lax.broadcasted_iota(jnp.int32, (heights, slots), 0)
        pick_ref[...] = jnp.transpose(jnp.where(height == slot_ref[...], 1.0, 0.0)).astype(jnp.bfloat16)

    for tile in range(tiles):
        start = tile * LANES
        width = min(LANES, heights - start)
        piece = leg_ref[:, :, start : start + width].astype(jnp.float32)
        leg32_ref[tile, :, :width] = piece.reshape(length * GROUP, width)
    coef32_ref[...] = coef_ref[...].astype(jnp.float32).reshape(coef32_ref.shape)
    even = length - 1
    position = lax.broadcasted_iota(jnp.int32, (1, even), 1)

    def one_pair(member):
        low = wave_ref[base + member]
        cut = even - low
        pick_rows = pl.ds(member, even, stride=GROUP)
        leg = jnp.concatenate([leg32_ref[tile, pick_rows, :] for tile in range(tiles)], axis=1)
        leg = leg[:, :heights].astype(jnp.bfloat16)
        coef = jnp.transpose(coef32_ref[pick_rows, :]).astype(jnp.bfloat16)
        in_low = position < cut
        operand = []
        for segment in range(2):
            keep = in_low if segment == 0 else jnp.logical_not(in_low)
            parity = lax.rem(position if segment == 0 else position + cut, 2)
            north = jnp.where(keep, 1.0, 0.0)
            south = jnp.where(parity == 0, north, -north).astype(jnp.bfloat16)
            north = north.astype(jnp.bfloat16)
            for part in range(2):
                values = coef[part * fields : (part + 1) * fields]
                operand += [values * north, values * south]
        operand = jnp.concatenate(operand, axis=0)
        fourier = jnp.dot(operand, leg, preferred_element_type=jnp.float32)
        last_row = pl.ds(even * GROUP + member, 1)
        last_leg = jnp.concatenate([leg32_ref[tile, last_row, :] for tile in range(tiles)], axis=1)
        last_coef = jnp.transpose(coef32_ref[last_row, :])
        sign = jnp.where(lax.rem(low, 2) == 0, 1.0, -1.0)
        halves = [last_coef[:fields], last_coef[fields:]]
        last = jnp.concatenate([v for h in halves for v in (h, h * sign)], axis=0)
        high = fourier[2 * columns :] + last * last_leg[:, :heights]
        fourier = jnp.concatenate([fourier[: 2 * columns], high], axis=0).astype(jnp.bfloat16)
        taken = lax.dot_general(
            pick_ref[...], fourier, (((1,), (1,)), ((), ())), preferred_element_type=jnp.float32
        )
        for kind in range(4):
            rows_ref[kind, pl.ds(member, slots, stride=GROUP), :] = taken[
                :, kind * columns : (kind + 1) * columns
            ]

    @pl.loop(0, GROUP // unroll)
    def _(step):
        for turn in range(unroll):
            one_pair(step * unroll + turn)

    for kind in range(4):
        out_ref[:, kind] = rows_ref[kind].reshape(slots, GROUP, columns).astype(jnp.bfloat16)


def legendre_rows(m_of_pair, row_of_slot, legendre, coef, first, groups, unroll):
    length, pairs_dev, heights = legendre.shape
    columns = coef.shape[2]
    slots = row_of_slot.shape[0]
    pairs = groups * GROUP
    return pl.pallas_call(
        functools.partial(
            legendre_kernel, length=length, first=first, pairs_dev=pairs_dev, unroll=unroll
        ),
        out_shape=jax.ShapeDtypeStruct((slots, 4, pairs, columns), jnp.bfloat16),
        grid_spec=pltpu.PrefetchScalarGridSpec(
            num_scalar_prefetch=1,
            grid=(groups,),
            in_specs=[
                pl.BlockSpec((1, slots), lambda group, wave: (0, 0)),
                pl.BlockSpec((length, GROUP, heights), lambda group, wave: (0, first + group, 0)),
                pl.BlockSpec((length, GROUP, columns), lambda group, wave: (0, first + group, 0)),
            ],
            out_specs=pl.BlockSpec((slots, 4, GROUP, columns), lambda group, wave: (0, 0, group, 0)),
            scratch_shapes=[
                pltpu.VMEM((slots, heights), jnp.bfloat16),
                pltpu.VMEM((pl.cdiv(heights, LANES), length * GROUP, LANES), jnp.float32),
                pltpu.VMEM((length * GROUP, columns), jnp.float32),
                pltpu.VMEM((4, slots * GROUP, columns), jnp.float32),
            ],
        ),
        compiler_params=pltpu.CompilerParams(vmem_limit_bytes=56 << 20),
        cost_estimate=pl.CostEstimate(
            flops=2 * pairs * 4 * columns * heights * (length + slots),
            bytes_accessed=2 * pairs * (length * (heights + columns) + slots * 4 * columns),
            transcendentals=0,
        ),
    )(m_of_pair, row_of_slot[None, :], legendre, coef)


def legendre_rows_plain(low_m, row_of_slot, legendre, coef):
    length = legendre.shape[0]
    fields = coef.shape[2] // 2
    position = jnp.arange(length, dtype=jnp.int32)[:, None]
    cut = (length - 1 - low_m)[None, :]
    in_low = position < cut
    parity = jnp.where(in_low, position, position + cut) % 2
    sign = jnp.where(parity == 0, 1.0, -1.0).astype(jnp.bfloat16)[:, :, None]
    kinds = []
    for keep in (in_low, ~in_low):
        kept = jnp.where(keep[:, :, None], coef, jnp.zeros((), coef.dtype))
        for part in range(2):
            values = kept[:, :, part * fields : (part + 1) * fields]
            kinds.append(jnp.concatenate([values, values * sign], axis=2))
    fourier = jnp.einsum(
        "kph,kpqc->hqpc", legendre, jnp.stack(kinds, axis=2), preferred_element_type=jnp.float32
    ).astype(jnp.bfloat16)
    taken = jnp.take(fourier, jnp.maximum(row_of_slot, 0), axis=0)
    return jnp.where((row_of_slot >= 0)[:, None, None, None], taken, jnp.zeros((), taken.dtype))


def dft_kernel(*refs, total):
    rows_ref, table_ref, *added, out_ref = refs
    for slot in range(out_ref.shape[0]):
        rows = rows_ref[:, slot].reshape(table_ref.shape[0], rows_ref.shape[3])
        values = lax.dot_general(
            rows, table_ref[...], (((0,), (0,)), ((), ())), preferred_element_type=jnp.float32
        ).reshape(out_ref.shape[1:])
        if total:
            values = values + added[0][slot]
        out_ref[slot] = values.astype(out_ref.dtype)


def dft_rows(rows, table, begin, *added, step=2):
    sources, slots, depth, columns = rows.shape
    depth = depth * sources
    total = bool(added)
    out_block = (step, 2, columns // 2, table.shape[1])
    out_spec = pl.BlockSpec(out_block, lambda block: (block, 0, 0, 0))
    return pl.pallas_call(
        functools.partial(dft_kernel, total=total),
        out_shape=jax.ShapeDtypeStruct(
            (slots,) + out_block[1:], jnp.bfloat16 if total else jnp.float32
        ),
        grid=(pl.cdiv(slots, step),),
        in_specs=[
            pl.BlockSpec((sources, step) + rows.shape[2:], lambda block: (0, block, 0, 0)),
            pl.BlockSpec(
                (depth, table.shape[1]),
                lambda block: (begin // depth, 0),
                pipeline_mode=pl.Buffered(1),
            ),
        ]
        + [out_spec] * len(added),
        out_specs=out_spec,
        compiler_params=pltpu.CompilerParams(vmem_limit_bytes=58 << 20),
        cost_estimate=pl.CostEstimate(
            flops=2 * slots * columns * depth * table.shape[1],
            bytes_accessed=2 * rows.size + (2 * depth + 6 * slots * columns) * table.shape[1],
            transcendentals=0,
        ),
    )(rows, table, *added)


def dft_rows_plain(rows, table):
    sources, slots, depth, columns = rows.shape
    values = jnp.einsum(
        "dlkc,dkj->lcj", rows, table.reshape(sources, depth, -1), preferred_element_type=jnp.float32
    )
    return values.astype(jnp.bfloat16).reshape(slots, 2, columns // 2, -1)


def dft_table(m_of_pair, wave_count, pairs_dev, cuts):
    low = m_of_pair.reshape(-1, 1, 1, pairs_dev)
    wave = jnp.concatenate([low, wave_count - 1 - low], axis=1)
    wave = jnp.broadcast_to(wave, (wave.shape[0], 2, 2, pairs_dev))
    shift = jnp.broadcast_to(jnp.array([0, NLON // 4], jnp.int32)[:, None], wave.shape)
    order = lambda values: jnp.concatenate(
        [values[..., begin:end].reshape(-1) for begin, end in cuts]
    )[:, None]
    wave, shift = order(wave), order(shift)
    longitude = jnp.arange(NLON, dtype=jnp.int32)
    angles = ((wave * longitude + shift) % NLON).astype(jnp.float32) * (2.0 * math.pi / NLON)
    weights = jnp.where(wave == 0, 1.0, 2.0).astype(jnp.float32)
    return (weights * jnp.cos(angles)).astype(jnp.bfloat16)


def dft_table_plain(m_of_pair, wave_count, pairs_dev):
    low = m_of_pair.reshape(-1, 1, pairs_dev)
    wave = jnp.concatenate([low, wave_count - 1 - low], axis=1)[..., None]
    longitude = jnp.arange(NLON, dtype=jnp.int32)
    angles = (wave * longitude % NLON).astype(jnp.float32) * (2.0 * math.pi / NLON)
    weights = jnp.where(wave == 0, 1.0, 2.0).astype(jnp.float32)
    table = jnp.stack([weights * jnp.cos(angles), -weights * jnp.sin(angles)], axis=2)
    return table.astype(jnp.bfloat16).reshape(-1, NLON)


def spectrum_terms(coef, low_m):
    pairs_dev, length, columns = coef.shape
    wave_count = length - 1
    fields = columns // 2
    squares = coef.astype(jnp.float32) ** 2
    power_sum = squares[:, :, :fields] + squares[:, :, fields:]
    padded = jnp.concatenate(
        [jnp.zeros((pairs_dev, wave_count, fields), jnp.float32), power_sum[:, :wave_count]], axis=1
    )
    shifted = jax.vmap(
        lambda values, offset: lax.dynamic_slice_in_dim(values, offset, wave_count, 0)
    )(padded, wave_count - low_m)
    degree = jnp.arange(wave_count, dtype=jnp.int32)
    high_keep = (degree[None, :] >= (wave_count - 1 - low_m)[:, None]).astype(jnp.float32)
    high_terms = power_sum[:, 1:] * high_keep[:, :, None]
    low_weight = jnp.where(low_m == 0, 1.0, 2.0).astype(jnp.float32)
    return jnp.sum(low_weight[:, None, None] * shifted + 2.0 * high_terms, axis=0)


def spectrum_kernel(wave_ref, coef_ref, out_ref, coef32_ref, low_ref, high_ref, *, pairs_dev):
    group = pl.program_id(0)
    base = lax.axis_index("lat") * pairs_dev + group * GROUP
    length, _, columns = coef_ref.shape
    wave_count = length - 1

    @pl.when(group == 0)
    def _():
        low_ref[...] = jnp.zeros_like(low_ref)
        high_ref[...] = jnp.zeros_like(high_ref)

    coef32_ref[...] = coef_ref[...].astype(jnp.float32).reshape(coef32_ref.shape)
    position = lax.broadcasted_iota(jnp.int32, (length, columns), 0)

    @pl.loop(0, GROUP)
    def _(member):
        low = wave_ref[base + member]
        values = coef32_ref[pl.ds(member, length, stride=GROUP), :]
        power = values * values
        in_low = position < wave_count - low
        weight = jnp.where(low == 0, 1.0, 2.0)
        low_ref[pl.ds(low, length), :] += jnp.where(in_low, weight * power, 0.0)
        high_ref[...] += jnp.where(in_low, 0.0, 2.0 * power)

    @pl.when(group == pl.num_programs(0) - 1)
    def _():
        terms = low_ref[pl.ds(0, wave_count), :] + high_ref[pl.ds(1, wave_count), :]
        terms = terms + pltpu.roll(terms, columns // 2, 1)
        out_ref[...] = terms[:, : columns // 2]


def spectrum_sums(m_of_pair, coef):
    length, pairs_dev, columns = coef.shape
    spare = length + (m_of_pair.shape[0] + 7) // 8 * 8
    return pl.pallas_call(
        functools.partial(spectrum_kernel, pairs_dev=pairs_dev),
        out_shape=jax.ShapeDtypeStruct((length - 1, columns // 2), jnp.float32),
        grid_spec=pltpu.PrefetchScalarGridSpec(
            num_scalar_prefetch=1,
            grid=(pairs_dev // GROUP,),
            in_specs=[pl.BlockSpec((length, GROUP, columns), lambda group, wave: (0, group, 0))],
            out_specs=pl.BlockSpec((length - 1, columns // 2), lambda group, wave: (0, 0)),
            scratch_shapes=[
                pltpu.VMEM((length * GROUP, columns), jnp.float32),
                pltpu.VMEM((spare, columns), jnp.float32),
                pltpu.VMEM((length, columns), jnp.float32),
            ],
        ),
        compiler_params=pltpu.CompilerParams(vmem_limit_bytes=24 << 20),
        cost_estimate=pl.CostEstimate(
            flops=8 * coef.size, bytes_accessed=2 * coef.size, transcendentals=0
        ),
    )(m_of_pair, coef)


def scale_kernel(summed_ref, after_ref, out_ref, *, wave_count):
    rows = summed_ref.shape[0]
    first = lax.axis_index("lat") * rows
    degree = (first + lax.broadcasted_iota(jnp.int32, summed_ref.shape, 0)).astype(jnp.float32)
    out_ref[...] = summed_ref[...] * (wave_count / (2.0 * degree + 1.0))


def spectrum_scale(summed, after, wave_count):
    whole = pl.BlockSpec(summed.shape, lambda: (0, 0))
    return pl.pallas_call(
        functools.partial(scale_kernel, wave_count=wave_count),
        out_shape=jax.ShapeDtypeStruct(summed.shape, summed.dtype),
        in_specs=[whole, pl.BlockSpec(memory_space=pl.ANY)],
        out_specs=whole,
    )(summed, after)


def exchange(outgoing, sources):
    incoming = lax.all_to_all(
        outgoing.reshape(outgoing.shape[0], -1, outgoing.shape[3]), "lat", split_axis=0, concat_axis=0, tiled=True
    )
    return incoming.reshape((sources, -1) + incoming.shape[1:])


def local(coef, legendre, m_of_pair, row_of_slot):
    pairs_dev, length, columns = coef.shape
    wave_count = length - 1
    device = lax.axis_index("lat")
    sources = m_of_pair.shape[0] // pairs_dev
    low_m = lax.dynamic_slice_in_dim(m_of_pair, device * pairs_dev, pairs_dev)
    legend_rows = jnp.transpose(legendre, (1, 0, 2))
    coef_rows = jnp.transpose(coef, (1, 0, 2))
    if pairs_dev % GROUP == 0 and pairs_dev > GROUP:
        groups = pairs_dev // GROUP
        rest = pairs_dev - GROUP
        head = functools.partial(legendre_rows, m_of_pair, row_of_slot, legend_rows, coef_rows)
        first_in = exchange(head(groups - 1, 1, 4), sources)
        second_in = exchange(head(0, groups - 1, 2), sources)
        table = dft_table(m_of_pair, wave_count, pairs_dev, ((0, rest), (rest, pairs_dev)))
        partial = dft_rows(first_in, table, 4 * sources * rest)
        grid_out = dft_rows(second_in, table, 0, partial)
        coef_rows, _ = lax.optimization_barrier((coef_rows, first_in[0, 0, 0, 0]))
        terms = spectrum_sums(m_of_pair, coef_rows)
        summed = lax.psum_scatter(terms, "lat", scatter_dimension=0, tiled=True)
        spectrum = spectrum_scale(summed, partial, wave_count)
    else:
        outgoing = legendre_rows_plain(low_m, row_of_slot, legend_rows, coef_rows)
        table = dft_table_plain(m_of_pair, wave_count, pairs_dev)
        grid_out = dft_rows_plain(exchange(outgoing, sources), table)
        terms = spectrum_terms(coef, low_m)
        summed = lax.psum_scatter(terms, "lat", scatter_dimension=0, tiled=True)
        local_degree = (
            device * summed.shape[0] + jnp.arange(summed.shape[0], dtype=jnp.int32)
        ).astype(jnp.float32)
        spectrum = summed * (wave_count / (2.0 * local_degree + 1.0))[:, None]
    return (grid_out, spectrum)


def solution(mesh):
    in_specs = (P("lat", None, "slab"), P("lat", None, None), P(), P())
    out_specs = (P("lat", None, "slab", None), P("lat", "slab"))
    return jax.shard_map(local, mesh=mesh, in_specs=in_specs, out_specs=out_specs, check_vma=False)
```

time: 277 us -> 263 us (0.949)
  local copies, waits for them, and re-layouts: 39.6 us -> 4.36 us
  Pallas kernels: 51.6 us -> 79.7 us
  other arithmetic: 55.3 us -> 41.1 us
  starting transfers between devices: 6.59 us -> 11.7 us
    convert_element_type x1, other arithmetic: 0.04 us -> 41.1 us  [dft_table(): return (weights * jnp.cos(angles)).astype(jnp.bfloat16)]
    all_to_all x1 -> x2, waiting for transfers between devices: 30.2 us -> 69.7 us  [exchange(): lax.all_to_all(outgoing.reshape(outgoing.shape[0], -1, outgoing.shape[3])...]
    reduce_scatter x1, waiting for transfers between devices: 78.8 us -> 41.4 us  [local(): summed = lax.psum_scatter(terms, 'lat', scatter_dimension=0, tiled=True)]
    pallas_call x2 -> x6, Pallas kernels: 51.6 us -> 79.7 us  [the longest x2 37.3 us: legendre_rows(): pl.pallas_call(functools.partial(legendre_kernel, length=length, first=fi...]
    another operation x2 -> x1, other arithmetic: 23.9 us -> 0.01 us
    gather x1 -> x0, local copies, waits for them, and re-layouts: 23.8 us -> none  [spectrum_terms(): lax.dynamic_slice_in_dim(values, offset, wave_count, 0)]
    add x1 -> x0, other arithmetic: 12.7 us -> none  [spectrum_terms(): power_sum = squares[:, :, :fields] + squares[:, :, fields:]]
    reduce_sum x1 -> x0, other arithmetic: 9.24 us -> none  [spectrum_terms(): jnp.sum(low_weight[:, None, None] * shifted + 2.0 * high_terms, axis=0)]
  transfers between devices with their start and end apart: 2 -> 3, of which waited for: 2 -> 3; matrix products, arithmetic and copies ran while one was open for 31% -> 16% of each run, Pallas kernels for 0% -> 17%
where the time goes in v1:
time: 263 us; the launch traced here: 262 us
  waiting for transfers between devices  111 us (42%)
  Pallas kernels  79.7 us (30%)
  other arithmetic  41.1 us (16%)
  between operations  14.1 us (5%)
  starting transfers between devices  11.7 us (4%)
  local copies, waits for them, and re-layouts  4.36 us (2%)
    all_to_all x2, waiting for transfers between devices, exchange(): lax.all_to_all(outgoing.reshape(outgoing.shape[0], -1, outgoing.shape[3])...  69.7 us
    reduce_scatter x1, waiting for transfers between devices, local(): summed = lax.psum_scatter(terms, 'lat', scatter_dimension=0, tiled=True)  41.4 us
    convert_element_type x1, other arithmetic, dft_table(): return (weights * jnp.cos(angles)).astype(jnp.bfloat16)  41.1 us
    pallas_call x2, Pallas kernels, legendre_rows(): pl.pallas_call(functools.partial(legendre_kernel, length=length, first=fi...  37.3 us
    pallas_call x2, Pallas kernels, dft_rows(): pl.pallas_call(functools.partial(dft_kernel, total=total), out_shape=jax....  33.6 us
    all_to_all x2, starting transfers between devices, exchange(): lax.all_to_all(outgoing.reshape(outgoing.shape[0], -1, outgoing.shape[3])...  11.5 us
    pallas_call x1, Pallas kernels, spectrum_sums(): pl.pallas_call(functools.partial(spectrum_kernel, pairs_dev=pairs_dev), o...  7.42 us
  transfers between devices with their start and end apart: 3, of which 3 were waited for; matrix products, arithmetic and copies ran while one was open for 16% of the time, Pallas kernels for 17%

profile of v1, /device:TPU:15, one launch (start us, length us, event | category | flops | bytes accessed | tf_op | source)
XLA Modules:
  0.0 262.0 jit_solution(12670570143316486515)
XLA Ops:
  7.2 1.2 broadcast_in_dim.28.slot_ref
  8.4 13.8 %shard_map.69 = bf16[368,4,8,128]{3,2,1,0:T(8,128)(2,1)} custom-call(s32[384]{0:T(512)} %wave_ref.5, s32[1,368]{1,0:T(1,128)} %broadcast_in_dim.28.slot_ref, bf16[769,24,360]{2,1,0:T(8,128)(2,1)} %bitcast.12, bf16[769,24,128]{2,1,0:T(8,128)(2,1)} %bitcast.9), custom_call_target="tpu_custom_call" | custom-call | flops 3353149440 | bytes 9019008 | tf_op jit(solution)/shard_map/pallas_call | solution.py:90
  22.2 6.6 %all-to-all-start.1 = ((bf16[368,32,128]{2,1,0:T(8,128)(2,1)}), bf16[368,32,128]{2,1,0:T(8,128)(2,1)S(1)}, u32[]{:S(2)}, u32[]{:S(2)}) async-start(bf16[368,32,128]{2,1,0:T(8,128)(2,1)} %bitcast.16), calls=%async_computation.1 | async-start | bytes 6029312 | tf_op jit(solution)/shard_map/all_to_all | solution.py:309
  28.8 23.5 %shard_map.68 = bf16[368,4,16,128]{3,2,1,0:T(8,128)(2,1)} custom-call(s32[384]{0:T(512)} %wave_ref.5, s32[1,368]{1,0:T(1,128)} %broadcast_in_dim.28.slot_ref, bf16[769,24,360]{2,1,0:T(8,128)(2,1)} %bitcast.13, bf16[769,24,128]{2,1,0:T(8,128)(2,1)} %bitcast.10), custom_call_target="tpu_custom_call" | custom-call | flops 6706298880 | bytes 18038016 | tf_op jit(solution)/shard_map/pallas_call | solution.py:90
  52.3 43.6 %all-to-all-done.1 = bf16[368,32,128]{2,1,0:T(8,128)(2,1)S(1)} async-done(((bf16[368,32,128]{2,1,0:T(8,128)(2,1)}), bf16[368,32,128]{2,1,0:T(8,128)(2,1)S(1)}, u32[]{:S(2)}, u32[]{:S(2)}) %all-to-all-start.1) | async-done | bytes 3014688 | tf_op jit(solution)/shard_map/all_to_all | solution.py:309
  95.8 4.9 %all-to-all-start = ((bf16[368,64,128]{2,1,0:T(8,128)(2,1)}), bf16[368,64,128]{2,1,0:T(8,128)(2,1)}, u32[]{:S(2)}, u32[]{:S(2)}) async-start(bf16[368,64,128]{2,1,0:T(8,128)(2,1)} %bitcast.14), calls=%async_computation | async-start | bytes 12058624 | tf_op jit(solution)/shard_map/all_to_all | solution.py:309
  100.8 0.2 reduce-scatter.2.cloned.1.call-start
  101.0 2.3 copy-done
  103.3 7.4 %shard_map.72 = f32[768,64]{1,0:T(8,128)} custom-call(s32[384]{0:T(512)S(1)} %copy-done.1, bf16[769,24,128]{2,1,0:T(8,128)(2,1)S(1)} %bitcast.11), custom_call_target="tpu_custom_call" | custom-call | flops 18898944 | bytes 4724736 | tf_op jit(solution)/shard_map/pallas_call | solution.py:270
  110.8 0.0 reduce-scatter.2.cloned.1.call-update
  110.8 0.1 reshape.63
  110.9 0.1 slice.20
  111.0 0.1 concatenate.19
  111.1 0.1 concatenate.18
  111.2 0.1 slice.17
  111.3 0.1 reshape.64
  111.4 0.1 slice.18
  111.5 0.1 reshape.65
  111.7 41.1 %fusion.4.refs_1_ = bf16[1536,1440]{1,0:T(8,128)(2,1)} fusion(s32[1536]{0:T(1024)S(1)} %pad_add_fusion, s32[1536]{0:T(1024)S(1)} %constant_dynamic-update-slice_fusion, f32[1536]{0:T(1024)S(1)} %compare_select_fusion), kind=kLoop, calls=%fused_computation.5 | loop fusion | flops 26542080 | bytes 4442112 | tf_op jit(solution)/shard_map/convert_element_type | solution.py:204
  152.7 13.5 %shard_map.70.refs_2_.after_ref = f32[23,2,64,1440]{3,2,1,0:T(8,128)} custom-call(bf16[16,23,32,128]{3,2,1,0:T(8,128)(2,1)} %bitcast.15, bf16[1536,1440]{1,0:T(8,128)(2,1)} %fusion.4.refs_1_), custom_call_target="tpu_custom_call" | custom-call | flops 4341104640 | bytes 29925376 | tf_op jit(solution)/shard_map/pallas_call | solution.py:159
  166.2 41.4 %reduce-scatter.2.cloned.1.call-done.summed_ref = f32[48,64]{1,0:T(8,128)} async-done(((f32[768,64]{1,0:T(8,128)}), f32[48,64]{1,0:T(8,128)}) %reduce-scatter.2.cloned.1.call-update) | async-done | bytes 12304 | tf_op jit(solution)/shard_map/reduce_scatter | solution.py:334
  207.6 1.4 shard_map.73
  209.0 26.1 %all-to-all-done = bf16[368,64,128]{2,1,0:T(8,128)(2,1)} async-done(((bf16[368,64,128]{2,1,0:T(8,128)(2,1)}), bf16[368,64,128]{2,1,0:T(8,128)(2,1)}, u32[]{:S(2)}, u32[]{:S(2)}) %all-to-all-start) | async-done | bytes 6029344 | tf_op jit(solution)/shard_map/all_to_all | solution.py:309
  235.1 20.1 %shard_map.71 = bf16[23,2,64,1440]{3,2,1,0:T(8,128)(2,1)} custom-call(bf16[16,23,64,128]{3,2,1,0:T(8,128)(2,1)} %bitcast.3.refs_0_, bf16[1536,1440]{1,0:T(8,128)(2,1)} %fusion.4.refs_1_, f32[23,2,64,1440]{3,2,1,0:T(8,128)} %shard_map.70.refs_2_.after_ref), custom_call_target="tpu_custom_call" | custom-call | flops 8682209280 | bytes 34414592 | tf_op jit(solution)/shard_map/pallas_call | solution.py:159
  (14 shorter events, 0.1 us)
Async XLA Ops:
  22.2 73.6 %all-to-all-start.1 = ((bf16[368,32,128]{2,1,0:T(8,128)(2,1)}), bf16[368,32,128]{2,1,0:T(8,128)(2,1)S(1)}, u32[]{:S(2)}, u32[]{:S(2)}) async-start(bf16[368,32,128]{2,1,0:T(8,128)(2,1)} %bitcast.16), calls=%async_computation.1 | async-start | bytes 6029312 | tf_op jit(solution)/shard_map/all_to_all | solution.py:309
  52.3 48.7 %copy-start.1 = (s32[384]{0:T(512)S(1)}, s32[384]{0:T(512)}, u32[]{:S(2)}) copy-start(s32[384]{0:T(512)} %wave_ref.5) | copy-start | bytes 4612
  95.8 56.9 %copy-start.2 = (bf16[368,32,128]{2,1,0:T(8,128)(2,1)}, bf16[368,32,128]{2,1,0:T(8,128)(2,1)S(1)}, u32[]{:S(2)}) copy-start(bf16[368,32,128]{2,1,0:T(8,128)(2,1)S(1)} %all-to-all-done.1) | copy-start | bytes 9043972
  95.8 139.2 %all-to-all-start = ((bf16[368,64,128]{2,1,0:T(8,128)(2,1)}), bf16[368,64,128]{2,1,0:T(8,128)(2,1)}, u32[]{:S(2)}, u32[]{:S(2)}) async-start(bf16[368,64,128]{2,1,0:T(8,128)(2,1)} %bitcast.14), calls=%async_computation | async-start | bytes 12058624 | tf_op jit(solution)/shard_map/all_to_all | solution.py:309
  100.8 106.9 %reduce-scatter.2.cloned.1.call-start = ((), (), s32[]{:S(2)}) async-start(), calls=%async_computation.3 | async-start | bytes 417792 | tf_op jit(solution)/shard_map/reduce_scatter | solution.py:334
  101.0 2.3 copy-start
Sparse Core Ops, SparseCore 0:
  110.9 96.6 reduce-scatter.1

commit v2 on v1

--- a/solution.py
+++ b/solution.py
@@ -150,7 +150,7 @@
         out_ref[slot] = values.astype(out_ref.dtype)
 
 
-def dft_rows(rows, table, begin, *added, step=2):
+def dft_rows(rows, table, begin, *added, step=4):
     sources, slots, depth, columns = rows.shape
     depth = depth * sources
     total = bool(added)
@@ -233,7 +233,7 @@
     return jnp.sum(low_weight[:, None, None] * shifted + 2.0 * high_terms, axis=0)
 
 
-def spectrum_kernel(wave_ref, coef_ref, out_ref, coef32_ref, low_ref, high_ref, *, pairs_dev):
+def spectrum_kernel(wave_ref, coef_ref, after_ref, out_ref, coef32_ref, low_ref, high_ref, *, pairs_dev):
     group = pl.program_id(0)
     base = lax.axis_index("lat") * pairs_dev + group * GROUP
     length, _, columns = coef_ref.shape
@@ -264,7 +264,7 @@
         out_ref[...] = terms[:, : columns // 2]
 
 
-def spectrum_sums(m_of_pair, coef):
+def spectrum_sums(m_of_pair, coef, after):
     length, pairs_dev, columns = coef.shape
     spare = length + (m_of_pair.shape[0] + 7) // 8 * 8
     return pl.pallas_call(
@@ -273,7 +273,10 @@
         grid_spec=pltpu.PrefetchScalarGridSpec(
             num_scalar_prefetch=1,
             grid=(pairs_dev // GROUP,),
-            in_specs=[pl.BlockSpec((length, GROUP, columns), lambda group, wave: (0, group, 0))],
+            in_specs=[
+                pl.BlockSpec((length, GROUP, columns), lambda group, wave: (0, group, 0)),
+                pl.BlockSpec(memory_space=pl.ANY),
+            ],
             out_specs=pl.BlockSpec((length - 1, columns // 2), lambda group, wave: (0, 0)),
             scratch_shapes=[
                 pltpu.VMEM((length * GROUP, columns), jnp.float32),
@@ -281,28 +284,62 @@
                 pltpu.VMEM((length, columns), jnp.float32),
             ],
         ),
-        compiler_params=pltpu.CompilerParams(vmem_limit_bytes=24 << 20),
+        compiler_params=pltpu.CompilerParams(vmem_limit_bytes=58 << 20),
         cost_estimate=pl.CostEstimate(
             flops=8 * coef.size, bytes_accessed=2 * coef.size, transcendentals=0
         ),
-    )(m_of_pair, coef)
-
-
-def scale_kernel(summed_ref, after_ref, out_ref, *, wave_count):
-    rows = summed_ref.shape[0]
-    first = lax.axis_index("lat") * rows
-    degree = (first + lax.broadcasted_iota(jnp.int32, summed_ref.shape, 0)).astype(jnp.float32)
-    out_ref[...] = summed_ref[...] * (wave_count / (2.0 * degree + 1.0))
-
-
-def spectrum_scale(summed, after, wave_count):
-    whole = pl.BlockSpec(summed.shape, lambda: (0, 0))
-    return pl.pallas_call(
-        functools.partial(scale_kernel, wave_count=wave_count),
-        out_shape=jax.ShapeDtypeStruct(summed.shape, summed.dtype),
-        in_specs=[whole, pl.BlockSpec(memory_space=pl.ANY)],
+    )(m_of_pair, coef, after)
+
+
+def sum_kernel(own_ref, *refs, scale):
+    *got, _, out_ref = refs
+    summed = own_ref[...]
+    for piece in got:
+        summed = summed + piece[...]
+    if scale:
+        first = lax.axis_index("lat") * own_ref.shape[0]
+        degree = (first + lax.broadcasted_iota(jnp.int32, own_ref.shape, 0)).astype(jnp.float32)
+        summed = summed * (scale / (2.0 * degree + 1.0))
+    out_ref[...] = summed
+
+
+def sum_pieces(pieces, after, scale=0):
+    shape = pieces[0].shape
+    whole = pl.BlockSpec(shape, lambda: (0, 0))
+    return pl.pallas_call(
+        functools.partial(sum_kernel, scale=scale),
+        out_shape=jax.ShapeDtypeStruct(shape, pieces[0].dtype),
+        in_specs=[whole] * len(pieces) + [pl.BlockSpec(memory_space=pl.ANY)],
         out_specs=whole,
-    )(summed, after)
+        compiler_params=pltpu.CompilerParams(vmem_limit_bytes=58 << 20),
+    )(*pieces, after)
+
+
+def gate_kernel(*refs):
+    pass
+
+
+def gate(value, *others):
+    anywhere = pl.BlockSpec(memory_space=pl.ANY)
+    return pl.pallas_call(
+        gate_kernel,
+        out_shape=jax.ShapeDtypeStruct(value.shape, value.dtype),
+        in_specs=[anywhere] * (1 + len(others)),
+        out_specs=anywhere,
+        input_output_aliases={0: 0},
+        compiler_params=pltpu.CompilerParams(vmem_limit_bytes=58 << 20),
+    )(value, *others)
+
+
+def scatter_round(terms, sources, stride, members):
+    index = lax.axis_index("lat") // stride % members
+    blocks = terms.reshape((members, -1) + terms.shape[1:])
+    mine = lambda step: lax.dynamic_index_in_dim(blocks, index ^ step, 0, keepdims=False)
+    pieces = [mine(0)]
+    for step in range(1, members):
+        pairs = [(i, i ^ (step * stride)) for i in range(sources)]
+        pieces.append(lax.ppermute(mine(step), "lat", pairs))
+    return pieces
 
 
 def exchange(outgoing, sources):
@@ -320,19 +357,20 @@
     low_m = lax.dynamic_slice_in_dim(m_of_pair, device * pairs_dev, pairs_dev)
     legend_rows = jnp.transpose(legendre, (1, 0, 2))
     coef_rows = jnp.transpose(coef, (1, 0, 2))
-    if pairs_dev % GROUP == 0 and pairs_dev > GROUP:
+    if pairs_dev % GROUP == 0 and pairs_dev > GROUP and sources == 16:
         groups = pairs_dev // GROUP
         rest = pairs_dev - GROUP
         head = functools.partial(legendre_rows, m_of_pair, row_of_slot, legend_rows, coef_rows)
-        first_in = exchange(head(groups - 1, 1, 4), sources)
-        second_in = exchange(head(0, groups - 1, 2), sources)
+        outgoing = head(groups - 1, 1, 4)
+        first_in = exchange(outgoing, sources)
+        terms = spectrum_sums(m_of_pair, coef_rows, outgoing)
+        pieces = scatter_round(terms, sources, 4, sources // 4)
+        second_in = exchange(gate(head(0, groups - 1, 2), *pieces[1:]), sources)
         table = dft_table(m_of_pair, wave_count, pairs_dev, ((0, rest), (rest, pairs_dev)))
         partial = dft_rows(first_in, table, 4 * sources * rest)
         grid_out = dft_rows(second_in, table, 0, partial)
-        coef_rows, _ = lax.optimization_barrier((coef_rows, first_in[0, 0, 0, 0]))
-        terms = spectrum_sums(m_of_pair, coef_rows)
-        summed = lax.psum_scatter(terms, "lat", scatter_dimension=0, tiled=True)
-        spectrum = spectrum_scale(summed, partial, wave_count)
+        pieces = scatter_round(sum_pieces(pieces, partial), sources, 1, 4)
+        spectrum = sum_pieces(pieces, grid_out, wave_count)
     else:
         outgoing = legendre_rows_plain(low_m, row_of_slot, legend_rows, coef_rows)
         table = dft_table_plain(m_of_pair, wave_count, pairs_dev)

time: 263 us -> 255 us (0.970)
  between operations: 14.1 us -> 0.81 us
  starting transfers between devices: 11.7 us -> 16.7 us
  Pallas kernels: 79.7 us -> 76.5 us
    reduce_scatter x1 -> x0, waiting for transfers between devices: 41.4 us -> none  [local(): summed = lax.psum_scatter(terms, 'lat', scatter_dimension=0, tiled=True)]
    ppermute x0 -> x6, waiting for transfers between devices: none -> 39.3 us  [scatter_round(): pieces.append(lax.ppermute(mine(step), 'lat', pairs))]
    pallas_call x2, Pallas kernels: 33.6 us -> 28 us  [dft_rows(): pl.pallas_call(functools.partial(dft_kernel, total=total), out_shape=jax....]
    ppermute x0 -> x6, starting transfers between devices: none -> 4.8 us  [scatter_round(): pieces.append(lax.ppermute(mine(step), 'lat', pairs))]
    all_to_all x2, waiting for transfers between devices: 69.7 us -> 73.8 us  [exchange(): lax.all_to_all(outgoing.reshape(outgoing.shape[0], -1, outgoing.shape[3])...]
    squeeze x0 -> x2, local copies, waits for them, and re-layouts: none -> 3.09 us  [scatter_round(): lax.dynamic_index_in_dim(blocks, index ^ step, 0, keepdims=False)]
  transfers between devices with their start and end apart: 3 -> 8, of which waited for: 3 -> 4; matrix products, arithmetic and copies ran while one was open for 16% -> 18% of each run, Pallas kernels for 17% -> 24%
where the time goes in v2:
time: 255 us
  waiting for transfers between devices  113 us (44%)
  Pallas kernels  76.5 us (30%)
  other arithmetic  41.1 us (16%)
  starting transfers between devices  16.7 us (7%)
  local copies, waits for them, and re-layouts  6.36 us (2%)
    all_to_all x2, waiting for transfers between devices, exchange(): lax.all_to_all(outgoing.reshape(outgoing.shape[0], -1, outgoing.shape[3])...  73.8 us
    convert_element_type x1, other arithmetic, dft_table(): return (weights * jnp.cos(angles)).astype(jnp.bfloat16)  41.1 us
    ppermute x6, waiting for transfers between devices, scatter_round(): pieces.append(lax.ppermute(mine(step), 'lat', pairs))  39.3 us
    pallas_call x2, Pallas kernels, legendre_rows(): pl.pallas_call(functools.partial(legendre_kernel, length=length, first=fi...  37.2 us
    pallas_call x2, Pallas kernels, dft_rows(): pl.pallas_call(functools.partial(dft_kernel, total=total), out_shape=jax....  28 us
    all_to_all x2, starting transfers between devices, exchange(): lax.all_to_all(outgoing.reshape(outgoing.shape[0], -1, outgoing.shape[3])...  11.9 us
    pallas_call x1, Pallas kernels, spectrum_sums(): pl.pallas_call(functools.partial(spectrum_kernel, pairs_dev=pairs_dev), o...  8.13 us
  transfers between devices with their start and end apart: 8, of which 4 were waited for; matrix products, arithmetic and copies ran while one was open for 18% of the time, Pallas kernels for 24%

profile of v2, /device:TPU:15, one launch (start us, length us, event | category | flops | bytes accessed | tf_op | source)
XLA Modules:
  0.0 254.6 jit_solution(15374457471639781746)
XLA Ops:
  0.6 1.2 broadcast_in_dim.28.slot_ref
  1.9 13.7 %shard_map.69.after_ref = bf16[368,4,8,128]{3,2,1,0:T(8,128)(2,1)} custom-call(s32[384]{0:T(512)} %wave_ref.5, s32[1,368]{1,0:T(1,128)} %broadcast_in_dim.28.slot_ref, bf16[769,24,360]{2,1,0:T(8,128)(2,1)} %bitcast.27, bf16[769,24,128]{2,1,0:T(8,128)(2,1)} %bitcast.30), custom_call_target="tpu_custom_call" | custom-call | flops 3353149440 | bytes 9019008 | tf_op jit(solution)/shard_map/pallas_call | solution.py:90
  15.6 6.6 %all-to-all-start.1 = ((bf16[368,32,128]{2,1,0:T(8,128)(2,1)}), bf16[368,32,128]{2,1,0:T(8,128)(2,1)S(1)}, u32[]{:S(2)}, u32[]{:S(2)}) async-start(bf16[368,32,128]{2,1,0:T(8,128)(2,1)} %bitcast.33), calls=%async_computation.1 | async-start | bytes 6029312 | tf_op jit(solution)/shard_map/all_to_all | solution.py:346
  22.2 8.1 %shard_map.70 = f32[768,64]{1,0:T(8,128)} custom-call(s32[384]{0:T(512)} %wave_ref.5, bf16[769,24,128]{2,1,0:T(8,128)(2,1)} %bitcast.31, bf16[368,4,8,128]{3,2,1,0:T(8,128)(2,1)} %shard_map.69.after_ref), custom_call_target="tpu_custom_call" | custom-call | flops 18898944 | bytes 4724736 | tf_op jit(solution)/shard_map/pallas_call | solution.py:270
  30.3 1.7 dynamic-slice_bitcast_fusion
  32.0 0.3 collective-permute-start
  32.3 2.1 collective-permute-start.1
  34.7 23.5 %shard_map.68.refs_0_ = bf16[368,4,16,128]{3,2,1,0:T(8,128)(2,1)} custom-call(s32[384]{0:T(512)} %wave_ref.5, s32[1,368]{1,0:T(1,128)} %broadcast_in_dim.28.slot_ref, bf16[769,24,360]{2,1,0:T(8,128)(2,1)} %bitcast.28, bf16[769,24,128]{2,1,0:T(8,128)(2,1)} %bitcast.32), custom_call_target="tpu_custom_call" | custom-call | flops 6706298880 | bytes 18038016 | tf_op jit(solution)/shard_map/pallas_call | solution.py:90
  58.2 17.0 %collective-permute-done.refs_1_.refs_0_ = f32[192,64]{1,0:T(8,128)S(1)} collective-permute-done((f32[192,64]{1,0:T(8,128)S(1)}, f32[192,64]{1,0:T(8,128)S(1)}, u32[]{:S(2)}, u32[]{:S(2)}) %collective-permute-start) | collective-permute-done | bytes 49184 | tf_op jit(solution)/shard_map/ppermute | solution.py:341
  75.1 18.3 %collective-permute-done.1.refs_2_.refs_1_ = f32[192,64]{1,0:T(8,128)S(1)} collective-permute-done((f32[192,64]{1,0:T(8,128)S(1)}, f32[192,64]{1,0:T(8,128)S(1)}, u32[]{:S(2)}, u32[]{:S(2)}) %collective-permute-start.1) | collective-permute-done | bytes 49184 | tf_op jit(solution)/shard_map/ppermute | solution.py:341
  93.4 4.1 %collective-permute-done.2.refs_3_.refs_2_ = f32[192,64]{1,0:T(8,128)S(1)} collective-permute-done((f32[192,64]{1,0:T(8,128)S(1)}, f32[192,64]{1,0:T(8,128)S(1)}, u32[]{:S(2)}, u32[]{:S(2)}) %collective-permute-start.2) | collective-permute-done | bytes 49184 | tf_op jit(solution)/shard_map/ppermute | solution.py:341
  97.5 0.6 copy-done.3
  98.2 5.4 %all-to-all-start = ((bf16[368,64,128]{2,1,0:T(8,128)(2,1)}), bf16[368,64,128]{2,1,0:T(8,128)(2,1)}, u32[]{:S(2)}, u32[]{:S(2)}) async-start(bf16[368,64,128]{2,1,0:T(8,128)(2,1)} %bitcast.29), calls=%async_computation | async-start | bytes 12058624 | tf_op jit(solution)/shard_map/all_to_all | solution.py:346
  104.5 41.1 %fusion.4.refs_1_ = bf16[1536,1440]{1,0:T(8,128)(2,1)} fusion(s32[1536]{0:T(1024)S(1)} %pad_add_fusion, s32[1536]{0:T(1024)S(1)} %constant_dynamic-update-slice_fusion, f32[1536]{0:T(1024)S(1)} %compare_select_fusion), kind=kLoop, calls=%fused_computation.5 | loop fusion | flops 26542080 | bytes 4442112 | tf_op jit(solution)/shard_map/convert_element_type | solution.py:204
  145.5 10.8 %shard_map.72.refs_2_.refs_3_ = f32[23,2,64,1440]{3,2,1,0:T(8,128)} custom-call(bf16[16,23,32,128]{3,2,1,0:T(8,128)(2,1)} %bitcast.34, bf16[1536,1440]{1,0:T(8,128)(2,1)} %fusion.4.refs_1_), custom_call_target="tpu_custom_call" | custom-call | flops 4341104640 | bytes 29925376 | tf_op jit(solution)/shard_map/pallas_call | solution.py:159
  156.3 1.7 shard_map.74
  158.0 1.4 dynamic-slice_bitcast_fusion.4
  159.4 0.4 collective-permute-start.3
  159.8 0.3 collective-permute-start.4
  160.0 1.5 collective-permute-start.5
  161.6 73.8 %all-to-all-done = bf16[368,64,128]{2,1,0:T(8,128)(2,1)} async-done(((bf16[368,64,128]{2,1,0:T(8,128)(2,1)}), bf16[368,64,128]{2,1,0:T(8,128)(2,1)}, u32[]{:S(2)}, u32[]{:S(2)}) %all-to-all-start) | async-done | bytes 6029344 | tf_op jit(solution)/shard_map/all_to_all | solution.py:346
  235.3 17.3 %shard_map.73.refs_3_ = bf16[23,2,64,1440]{3,2,1,0:T(8,128)(2,1)} custom-call(bf16[16,23,64,128]{3,2,1,0:T(8,128)(2,1)} %bitcast.7.refs_0_, bf16[1536,1440]{1,0:T(8,128)(2,1)} %fusion.4.refs_1_, f32[23,2,64,1440]{3,2,1,0:T(8,128)} %shard_map.72.refs_2_.refs_3_), custom_call_target="tpu_custom_call" | custom-call | flops 8682209280 | bytes 34414592 | tf_op jit(solution)/shard_map/pallas_call | solution.py:159
  252.6 0.6 copy-done.5
  253.2 1.4 shard_map.75
  (37 shorter events, 1.2 us)
Async XLA Ops:
  15.6 82.5 %all-to-all-start.1 = ((bf16[368,32,128]{2,1,0:T(8,128)(2,1)}), bf16[368,32,128]{2,1,0:T(8,128)(2,1)S(1)}, u32[]{:S(2)}, u32[]{:S(2)}) async-start(bf16[368,32,128]{2,1,0:T(8,128)(2,1)} %bitcast.33), calls=%async_computation.1 | async-start | bytes 6029312 | tf_op jit(solution)/shard_map/all_to_all | solution.py:346
  32.0 43.1 %collective-permute-start = (f32[192,64]{1,0:T(8,128)S(1)}, f32[192,64]{1,0:T(8,128)S(1)}, u32[]{:S(2)}, u32[]{:S(2)}) collective-permute-start(f32[192,64]{1,0:T(8,128)S(1)} %get-tuple-element.5), channel_id=1, source_target_pairs={{0,4},{1,5},{2,6},{3,7},{4,0},{5,1},{6,2},{7,3},{8,12},{9,13},{10,... | collective-permute-start | bytes 147464 | tf_op jit(solution)/shard_map/ppermute | solution.py:341
  32.3 61.1 %collective-permute-start.1 = (f32[192,64]{1,0:T(8,128)S(1)}, f32[192,64]{1,0:T(8,128)S(1)}, u32[]{:S(2)}, u32[]{:S(2)}) collective-permute-start(f32[192,64]{1,0:T(8,128)S(1)} %get-tuple-element.4), channel_id=1, source_target_pairs={{0,8},{1,9},{2,10},{3,11},{4,12},{5,13},{6,14},{7,15},{8,0},{9,1},... | collective-permute-start | bytes 147464 | tf_op jit(solution)/shard_map/ppermute | solution.py:341
  34.4 63.1 %collective-permute-start.2 = (f32[192,64]{1,0:T(8,128)S(1)}, f32[192,64]{1,0:T(8,128)S(1)}, u32[]{:S(2)}, u32[]{:S(2)}) collective-permute-start(f32[192,64]{1,0:T(8,128)S(1)} %get-tuple-element.3), channel_id=1, source_target_pairs={{0,12},{1,13},{2,14},{3,15},{4,8},{5,9},{6,10},{7,11},{8,4},{9,5},... | collective-permute-start | bytes 147464 | tf_op jit(solution)/shard_map/ppermute | solution.py:341
  58.2 45.4 %copy-start.4 = (s32[384]{0:T(512)S(1)}, s32[384]{0:T(512)}, u32[]{:S(2)}) copy-start(s32[384]{0:T(512)} %wave_ref.5) | copy-start | bytes 4612
  75.1 22.4 %copy-start.1 = (f32[192,64]{1,0:T(8,128)}, f32[192,64]{1,0:T(8,128)S(1)}, u32[]{:S(2)}) copy-start(f32[192,64]{1,0:T(8,128)S(1)} %collective-permute-done.refs_1_.refs_0_) | copy-start | bytes 147460
  93.4 4.1 %copy-start.2 = (f32[192,64]{1,0:T(8,128)}, f32[192,64]{1,0:T(8,128)S(1)}, u32[]{:S(2)}) copy-start(f32[192,64]{1,0:T(8,128)S(1)} %collective-permute-done.1.refs_2_.refs_1_) | copy-start | bytes 147460
  97.5 0.6 copy-start.3
  98.2 47.4 %copy-start = (bf16[368,32,128]{2,1,0:T(8,128)(2,1)}, bf16[368,32,128]{2,1,0:T(8,128)(2,1)S(1)}, u32[]{:S(2)}) copy-start(bf16[368,32,128]{2,1,0:T(8,128)(2,1)S(1)} %all-to-all-done.1) | copy-start | bytes 9043972
  98.2 137.2 %all-to-all-start = ((bf16[368,64,128]{2,1,0:T(8,128)(2,1)}), bf16[368,64,128]{2,1,0:T(8,128)(2,1)}, u32[]{:S(2)}, u32[]{:S(2)}) async-start(bf16[368,64,128]{2,1,0:T(8,128)(2,1)} %bitcast.29), calls=%async_computation | async-start | bytes 12058624 | tf_op jit(solution)/shard_map/all_to_all | solution.py:346
  159.4 93.2 %collective-permute-start.3 = (f32[48,64]{1,0:T(8,128)S(1)}, f32[48,64]{1,0:T(8,128)S(1)}, u32[]{:S(2)}, u32[]{:S(2)}) collective-permute-start(f32[48,64]{1,0:T(8,128)S(1)} %get-tuple-element.8), channel_id=1, source_target_pairs={{0,1},{1,0},{2,3},{3,2},{4,5},{5,4},{6,7},{7,6},{8,9},{9,8},{10,11... | collective-permute-start | bytes 36872 | tf_op jit(solution)/shard_map/ppermute | solution.py:341
  159.8 92.8 %collective-permute-start.4 = (f32[48,64]{1,0:T(8,128)S(1)}, f32[48,64]{1,0:T(8,128)S(1)}, u32[]{:S(2)}, u32[]{:S(2)}) collective-permute-start(f32[48,64]{1,0:T(8,128)S(1)} %get-tuple-element.7), channel_id=1, source_target_pairs={{0,2},{1,3},{2,0},{3,1},{4,6},{5,7},{6,4},{7,5},{8,10},{9,11},{10,... | collective-permute-start | bytes 36872 | tf_op jit(solution)/shard_map/ppermute | solution.py:341
  160.0 92.6 %collective-permute-start.5 = (f32[48,64]{1,0:T(8,128)S(1)}, f32[48,64]{1,0:T(8,128)S(1)}, u32[]{:S(2)}, u32[]{:S(2)}) collective-permute-start(f32[48,64]{1,0:T(8,128)S(1)} %get-tuple-element.6), channel_id=1, source_target_pairs={{0,3},{1,2},{2,1},{3,0},{4,7},{5,6},{6,5},{7,4},{8,11},{9,10},{10,... | collective-permute-start | bytes 36872 | tf_op jit(solution)/shard_map/ppermute | solution.py:341
  252.6 0.6 copy-start.5
  252.6 0.6 copy-start.6
  252.6 0.6 copy-start.7

commit v3 on v2

--- a/solution.py
+++ b/solution.py
@@ -26,7 +26,7 @@
     @pl.when(group == 0)
     def _():
         height = lax.broadcasted_iota(jnp.int32, (heights, slots), 0)
-        pick_ref[...] = jnp.transpose(jnp.where(height == slot_ref[...], 1.0, 0.0)).astype(jnp.bfloat16)
+        pick_ref[...] = jnp.transpose(jnp.where(height == slot_ref[...].reshape(1, slots), 1.0, 0.0)).astype(jnp.bfloat16)
 
     for tile in range(tiles):
         start = tile * LANES
@@ -96,7 +96,7 @@
             num_scalar_prefetch=1,
             grid=(groups,),
             in_specs=[
-                pl.BlockSpec((1, slots), lambda group, wave: (0, 0)),
+                pl.BlockSpec((slots,), lambda group, wave: (0,)),
                 pl.BlockSpec((length, GROUP, heights), lambda group, wave: (0, first + group, 0)),
                 pl.BlockSpec((length, GROUP, columns), lambda group, wave: (0, first + group, 0)),
             ],
@@ -114,7 +114,7 @@
             bytes_accessed=2 * pairs * (length * (heights + columns) + slots * 4 * columns),
             transcendentals=0,
         ),
-    )(m_of_pair, row_of_slot[None, :], legendre, coef)
+    )(m_of_pair, row_of_slot, legendre, coef)
 
 
 def legendre_rows_plain(low_m, row_of_slot, legendre, coef):
@@ -315,31 +315,15 @@
     )(*pieces, after)
 
 
-def gate_kernel(*refs):
-    pass
-
-
-def gate(value, *others):
-    anywhere = pl.BlockSpec(memory_space=pl.ANY)
-    return pl.pallas_call(
-        gate_kernel,
-        out_shape=jax.ShapeDtypeStruct(value.shape, value.dtype),
-        in_specs=[anywhere] * (1 + len(others)),
-        out_specs=anywhere,
-        input_output_aliases={0: 0},
-        compiler_params=pltpu.CompilerParams(vmem_limit_bytes=58 << 20),
-    )(value, *others)
-
-
 def scatter_round(terms, sources, stride, members):
     index = lax.axis_index("lat") // stride % members
-    blocks = terms.reshape((members, -1) + terms.shape[1:])
-    mine = lambda step: lax.dynamic_index_in_dim(blocks, index ^ step, 0, keepdims=False)
+    axis = 1 if stride == 1 and terms.ndim == 4 else 0
+    mine = lambda step: lax.dynamic_index_in_dim(terms, index ^ step, axis, keepdims=False)
     pieces = [mine(0)]
     for step in range(1, members):
         pairs = [(i, i ^ (step * stride)) for i in range(sources)]
         pieces.append(lax.ppermute(mine(step), "lat", pairs))
-    return pieces
+    return [piece.reshape(-1, terms.shape[-1]) for piece in pieces]
 
 
 def exchange(outgoing, sources):
@@ -363,13 +347,15 @@
         head = functools.partial(legendre_rows, m_of_pair, row_of_slot, legend_rows, coef_rows)
         outgoing = head(groups - 1, 1, 4)
         first_in = exchange(outgoing, sources)
-        terms = spectrum_sums(m_of_pair, coef_rows, outgoing)
-        pieces = scatter_round(terms, sources, 4, sources // 4)
-        second_in = exchange(gate(head(0, groups - 1, 2), *pieces[1:]), sources)
+        second_in = exchange(head(0, groups - 1, 2), sources)
         table = dft_table(m_of_pair, wave_count, pairs_dev, ((0, rest), (rest, pairs_dev)))
         partial = dft_rows(first_in, table, 4 * sources * rest)
         grid_out = dft_rows(second_in, table, 0, partial)
-        pieces = scatter_round(sum_pieces(pieces, partial), sources, 1, 4)
+        terms = spectrum_sums(m_of_pair, coef_rows, outgoing)
+        terms = terms.reshape(sources // 4, 4, -1, columns // 2)
+        terms = sum_pieces(scatter_round(terms, sources, 1, 4), partial)
+        terms = terms.reshape(sources // 4, -1, columns // 2)
+        pieces = scatter_round(terms, sources, 4, sources // 4)
         spectrum = sum_pieces(pieces, grid_out, wave_count)
     else:
         outgoing = legendre_rows_plain(low_m, row_of_slot, legend_rows, coef_rows)

time: 255 us -> 246 us (0.965)
  waiting for transfers between devices: 113 us -> 106 us
    ppermute x6, waiting for transfers between devices: 39.3 us -> 0.02 us  [scatter_round(): pieces.append(lax.ppermute(mine(step), 'lat', pairs))]
    all_to_all x2, waiting for transfers between devices: 73.8 us -> 106 us  [exchange(): lax.all_to_all(outgoing.reshape(outgoing.shape[0], -1, outgoing.shape[3])...]
  transfers between devices with their start and end apart: 8 -> 8, of which waited for: 4 -> 2; matrix products, arithmetic and copies ran while one was open for 18% -> 18% of each run, Pallas kernels for 24% -> 25%
where the time goes in v3:
time: 246 us
  waiting for transfers between devices  106 us (43%)
  Pallas kernels  76.7 us (31%)
  other arithmetic  41.1 us (17%)
  starting transfers between devices  16.4 us (7%)
  local copies, waits for them, and re-layouts  5.17 us (2%)
    all_to_all x2, waiting for transfers between devices, exchange(): lax.all_to_all(outgoing.reshape(outgoing.shape[0], -1, outgoing.shape[3])...  106 us
    convert_element_type x1, other arithmetic, dft_table(): return (weights * jnp.cos(angles)).astype(jnp.bfloat16)  41.1 us
    pallas_call x2, Pallas kernels, legendre_rows(): pl.pallas_call(functools.partial(legendre_kernel, length=length, first=fi...  37.4 us
    pallas_call x2, Pallas kernels, dft_rows(): pl.pallas_call(functools.partial(dft_kernel, total=total), out_shape=jax....  28 us
    all_to_all x2, starting transfers between devices, exchange(): lax.all_to_all(outgoing.reshape(outgoing.shape[0], -1, outgoing.shape[3])...  11.6 us
    pallas_call x1, Pallas kernels, spectrum_sums(): pl.pallas_call(functools.partial(spectrum_kernel, pairs_dev=pairs_dev), o...  8.15 us
  transfers between devices with their start and end apart: 8, of which 2 were waited for; matrix products, arithmetic and copies ran while one was open for 18% of the time, Pallas kernels for 25%

profile of v3, /device:TPU:15, one launch (start us, length us, event | category | flops | bytes accessed | tf_op | source)
XLA Modules:
  0.0 245.8 jit_solution(2657201689231054148)
XLA Ops:
  0.6 13.8 %shard_map.69.after_ref = bf16[368,4,8,128]{3,2,1,0:T(8,128)(2,1)} custom-call(s32[384]{0:T(512)} %wave_ref.5, s32[368]{0:T(512)} %slot_ref.3, bf16[769,24,360]{2,1,0:T(8,128)(2,1)} %bitcast.31, bf16[769,24,128]{2,1,0:T(8,128)(2,1)} %bitcast.33), custom_call_target="tpu_custom_call" | custom-call | flops 3353149440 | bytes 9019008 | tf_op jit(solution)/shard_map/pallas_call | solution.py:90
  14.5 6.6 %all-to-all-start.1 = ((bf16[368,32,128]{2,1,0:T(8,128)(2,1)}), bf16[368,32,128]{2,1,0:T(8,128)(2,1)S(1)}, u32[]{:S(2)}, u32[]{:S(2)}) async-start(bf16[368,32,128]{2,1,0:T(8,128)(2,1)} %bitcast.36), calls=%async_computation.1 | async-start | bytes 6029312 | tf_op jit(solution)/shard_map/all_to_all | solution.py:330
  21.0 23.5 %shard_map.68 = bf16[368,4,16,128]{3,2,1,0:T(8,128)(2,1)} custom-call(s32[384]{0:T(512)} %wave_ref.5, s32[368]{0:T(512)} %slot_ref.3, bf16[769,24,360]{2,1,0:T(8,128)(2,1)} %bitcast.32, bf16[769,24,128]{2,1,0:T(8,128)(2,1)} %bitcast.34), custom_call_target="tpu_custom_call" | custom-call | flops 6706298880 | bytes 18038016 | tf_op jit(solution)/shard_map/pallas_call | solution.py:90
  44.5 43.6 %all-to-all-done.1 = bf16[368,32,128]{2,1,0:T(8,128)(2,1)S(1)} async-done(((bf16[368,32,128]{2,1,0:T(8,128)(2,1)}), bf16[368,32,128]{2,1,0:T(8,128)(2,1)S(1)}, u32[]{:S(2)}, u32[]{:S(2)}) %all-to-all-start.1) | async-done | bytes 3014688 | tf_op jit(solution)/shard_map/all_to_all | solution.py:330
  88.1 5.0 %all-to-all-start = ((bf16[368,64,128]{2,1,0:T(8,128)(2,1)}), bf16[368,64,128]{2,1,0:T(8,128)(2,1)}, u32[]{:S(2)}, u32[]{:S(2)}) async-start(bf16[368,64,128]{2,1,0:T(8,128)(2,1)} %bitcast.37), calls=%async_computation | async-start | bytes 12058624 | tf_op jit(solution)/shard_map/all_to_all | solution.py:330
  93.2 8.2 %shard_map.72 = f32[768,64]{1,0:T(8,128)} custom-call(s32[384]{0:T(512)} %wave_ref.5, bf16[769,24,128]{2,1,0:T(8,128)(2,1)} %bitcast.35, bf16[368,4,8,128]{3,2,1,0:T(8,128)(2,1)} %shard_map.69.after_ref), custom_call_target="tpu_custom_call" | custom-call | flops 18898944 | bytes 4724736 | tf_op jit(solution)/shard_map/pallas_call | solution.py:270
  101.3 1.7 dynamic-slice_bitcast_fusion
  103.0 0.4 collective-permute-start
  103.4 0.3 collective-permute-start.1
  103.7 1.5 collective-permute-start.2
  105.8 0.1 reshape.83
  105.9 0.1 reshape.84
  106.1 41.1 %fusion.4.refs_1_ = bf16[1536,1440]{1,0:T(8,128)(2,1)} fusion(s32[1536]{0:T(1024)S(1)} %pad_add_fusion, s32[1536]{0:T(1024)S(1)} %constant_dynamic-update-slice_fusion, f32[1536]{0:T(1024)S(1)} %compare_select_fusion), kind=kLoop, calls=%fused_computation.5 | loop fusion | flops 26542080 | bytes 4442112 | tf_op jit(solution)/shard_map/convert_element_type | solution.py:204
  147.2 10.8 %shard_map.70.refs_2_.refs_3_ = f32[23,2,64,1440]{3,2,1,0:T(8,128)} custom-call(bf16[16,23,32,128]{3,2,1,0:T(8,128)(2,1)} %bitcast.38, bf16[1536,1440]{1,0:T(8,128)(2,1)} %fusion.4.refs_1_), custom_call_target="tpu_custom_call" | custom-call | flops 4341104640 | bytes 29925376 | tf_op jit(solution)/shard_map/pallas_call | solution.py:159
  158.0 0.6 copy-done.1
  158.7 1.7 shard_map.73
  160.4 1.4 dynamic-slice_bitcast_fusion.3
  161.8 0.3 collective-permute-start.3
  162.1 2.1 collective-permute-start.4
  164.2 0.3 collective-permute-start.5
  164.4 62.1 %all-to-all-done = bf16[368,64,128]{2,1,0:T(8,128)(2,1)} async-done(((bf16[368,64,128]{2,1,0:T(8,128)(2,1)}), bf16[368,64,128]{2,1,0:T(8,128)(2,1)}, u32[]{:S(2)}, u32[]{:S(2)}) %all-to-all-start) | async-done | bytes 6029344 | tf_op jit(solution)/shard_map/all_to_all | solution.py:330
  226.5 17.3 %shard_map.71.refs_3_ = bf16[23,2,64,1440]{3,2,1,0:T(8,128)(2,1)} custom-call(bf16[16,23,64,128]{3,2,1,0:T(8,128)(2,1)} %bitcast.3.refs_0_, bf16[1536,1440]{1,0:T(8,128)(2,1)} %fusion.4.refs_1_, f32[23,2,64,1440]{3,2,1,0:T(8,128)} %shard_map.70.refs_2_.refs_3_), custom_call_target="tpu_custom_call" | custom-call | flops 8682209280 | bytes 34414592 | tf_op jit(solution)/shard_map/pallas_call | solution.py:159
  243.8 0.6 copy-done.5
  244.4 1.4 shard_map.74
  (35 shorter events, 0.7 us)
Async XLA Ops:
  14.5 73.6 %all-to-all-start.1 = ((bf16[368,32,128]{2,1,0:T(8,128)(2,1)}), bf16[368,32,128]{2,1,0:T(8,128)(2,1)S(1)}, u32[]{:S(2)}, u32[]{:S(2)}) async-start(bf16[368,32,128]{2,1,0:T(8,128)(2,1)} %bitcast.36), calls=%async_computation.1 | async-start | bytes 6029312 | tf_op jit(solution)/shard_map/all_to_all | solution.py:330
  88.1 13.2 %copy-start = (bf16[368,32,128]{2,1,0:T(8,128)(2,1)}, bf16[368,32,128]{2,1,0:T(8,128)(2,1)S(1)}, u32[]{:S(2)}) copy-start(bf16[368,32,128]{2,1,0:T(8,128)(2,1)S(1)} %all-to-all-done.1) | copy-start | bytes 9043972
  88.1 17.1 %copy-start.4 = (s32[384]{0:T(512)S(1)}, s32[384]{0:T(512)}, u32[]{:S(2)}) copy-start(s32[384]{0:T(512)} %wave_ref.5) | copy-start | bytes 4612
  88.1 138.4 %all-to-all-start = ((bf16[368,64,128]{2,1,0:T(8,128)(2,1)}), bf16[368,64,128]{2,1,0:T(8,128)(2,1)}, u32[]{:S(2)}, u32[]{:S(2)}) async-start(bf16[368,64,128]{2,1,0:T(8,128)(2,1)} %bitcast.37), calls=%async_computation | async-start | bytes 12058624 | tf_op jit(solution)/shard_map/all_to_all | solution.py:330
  103.0 55.0 %collective-permute-start = (f32[4,48,64]{2,1,0:T(8,128)S(1)}, f32[4,48,64]{2,1,0:T(8,128)S(1)}, u32[]{:S(2)}, u32[]{:S(2)}) collective-permute-start(f32[4,48,64]{2,1,0:T(8,128)S(1)} %get-tuple-element.4), channel_id=1, source_target_pairs={{0,1},{1,0},{2,3},{3,2},{4,5},{5,4},{6,7},{7,6},{8,9},{9,8},{10,11... | collective-permute-start | bytes 147464 | tf_op jit(solution)/shard_map/ppermute | solution.py:325
  103.4 54.6 %collective-permute-start.1 = (f32[4,48,64]{2,1,0:T(8,128)S(1)}, f32[4,48,64]{2,1,0:T(8,128)S(1)}, u32[]{:S(2)}, u32[]{:S(2)}) collective-permute-start(f32[4,48,64]{2,1,0:T(8,128)S(1)} %get-tuple-element.3), channel_id=1, source_target_pairs={{0,2},{1,3},{2,0},{3,1},{4,6},{5,7},{6,4},{7,5},{8,10},{9,11},{10,... | collective-permute-start | bytes 147464 | tf_op jit(solution)/shard_map/ppermute | solution.py:325
  103.7 54.4 %collective-permute-start.2 = (f32[4,48,64]{2,1,0:T(8,128)S(1)}, f32[4,48,64]{2,1,0:T(8,128)S(1)}, u32[]{:S(2)}, u32[]{:S(2)}) collective-permute-start(f32[4,48,64]{2,1,0:T(8,128)S(1)} %get-tuple-element.2), channel_id=1, source_target_pairs={{0,3},{1,2},{2,1},{3,0},{4,7},{5,6},{6,5},{7,4},{8,11},{9,10},{10,... | collective-permute-start | bytes 147464 | tf_op jit(solution)/shard_map/ppermute | solution.py:325
  158.0 0.7 copy-start.1
  158.0 0.7 copy-start.2
  158.0 0.7 copy-start.3
  161.8 82.0 %collective-permute-start.3 = (f32[48,64]{1,0:T(8,128)S(1)}, f32[48,64]{1,0:T(8,128)S(1)}, u32[]{:S(2)}, u32[]{:S(2)}) collective-permute-start(f32[48,64]{1,0:T(8,128)S(1)} %get-tuple-element.8), channel_id=1, source_target_pairs={{0,4},{1,5},{2,6},{3,7},{4,0},{5,1},{6,2},{7,3},{8,12},{9,13},{10,... | collective-permute-start | bytes 36872 | tf_op jit(solution)/shard_map/ppermute | solution.py:325
  162.1 81.7 %collective-permute-start.4 = (f32[48,64]{1,0:T(8,128)S(1)}, f32[48,64]{1,0:T(8,128)S(1)}, u32[]{:S(2)}, u32[]{:S(2)}) collective-permute-start(f32[48,64]{1,0:T(8,128)S(1)} %get-tuple-element.7), channel_id=1, source_target_pairs={{0,8},{1,9},{2,10},{3,11},{4,12},{5,13},{6,14},{7,15},{8,0},{9,1},... | collective-permute-start | bytes 36872 | tf_op jit(solution)/shard_map/ppermute | solution.py:325
  164.2 79.6 %collective-permute-start.5 = (f32[48,64]{1,0:T(8,128)S(1)}, f32[48,64]{1,0:T(8,128)S(1)}, u32[]{:S(2)}, u32[]{:S(2)}) collective-permute-start(f32[48,64]{1,0:T(8,128)S(1)} %get-tuple-element.6), channel_id=1, source_target_pairs={{0,12},{1,13},{2,14},{3,15},{4,8},{5,9},{6,10},{7,11},{8,4},{9,5},... | collective-permute-start | bytes 36872 | tf_op jit(solution)/shard_map/ppermute | solution.py:325
  243.8 0.6 copy-start.5
  243.8 0.6 copy-start.6
  243.8 0.6 copy-start.7

commit v4 on v3

--- a/solution.py
+++ b/solution.py
@@ -10,12 +10,14 @@
 
 NLON = 1440
 GROUP = 8
+STEP = 4
 LANES = 128
 
 
 def legendre_kernel(
-    wave_ref, slot_ref, leg_ref, coef_ref, out_ref, pick_ref, leg32_ref, coef32_ref, rows_ref, *, length, first, pairs_dev, unroll
+    wave_ref, slot_ref, leg_ref, coef_ref, *refs, length, first, pairs_dev, unroll
 ):
+    *out_refs, pick_ref, leg32_ref, coef32_ref, rows_ref = refs
     group = pl.program_id(0)
     base = lax.axis_index("lat") * pairs_dev + (first + group) * GROUP
     slots, heights = pick_ref.shape
@@ -78,11 +80,16 @@
         for turn in range(unroll):
             one_pair(step * unroll + turn)
 
-    for kind in range(4):
-        out_ref[:, kind] = rows_ref[kind].reshape(slots, GROUP, columns).astype(jnp.bfloat16)
-
-
-def legendre_rows(m_of_pair, row_of_slot, legendre, coef, first, groups, unroll):
+    begin = 0
+    for out_ref in out_refs:
+        count = out_ref.shape[0]
+        for kind in range(4):
+            values = rows_ref[kind, begin * GROUP : (begin + count) * GROUP, :]
+            out_ref[:, kind] = values.reshape(count, GROUP, columns).astype(jnp.bfloat16)
+        begin += count
+
+
+def legendre_rows(m_of_pair, legendre, coef, row_of_slot, parts, first, groups, unroll):
     length, pairs_dev, heights = legendre.shape
     columns = coef.shape[2]
     slots = row_of_slot.shape[0]
@@ -91,7 +98,7 @@
         functools.partial(
             legendre_kernel, length=length, first=first, pairs_dev=pairs_dev, unroll=unroll
         ),
-        out_shape=jax.ShapeDtypeStruct((slots, 4, pairs, columns), jnp.bfloat16),
+        out_shape=[jax.ShapeDtypeStruct((part, 4, pairs, columns), jnp.bfloat16) for part in parts],
         grid_spec=pltpu.PrefetchScalarGridSpec(
             num_scalar_prefetch=1,
             grid=(groups,),
@@ -100,7 +107,10 @@
                 pl.BlockSpec((length, GROUP, heights), lambda group, wave: (0, first + group, 0)),
                 pl.BlockSpec((length, GROUP, columns), lambda group, wave: (0, first + group, 0)),
             ],
-            out_specs=pl.BlockSpec((slots, 4, GROUP, columns), lambda group, wave: (0, 0, group, 0)),
+            out_specs=[
+                pl.BlockSpec((part, 4, GROUP, columns), lambda group, wave: (0, 0, group, 0))
+                for part in parts
+            ],
             scratch_shapes=[
                 pltpu.VMEM((slots, heights), jnp.bfloat16),
                 pltpu.VMEM((pl.cdiv(heights, LANES), length * GROUP, LANES), jnp.float32),
@@ -138,28 +148,27 @@
     return jnp.where((row_of_slot >= 0)[:, None, None, None], taken, jnp.zeros((), taken.dtype))
 
 
-def dft_kernel(*refs, total):
-    rows_ref, table_ref, *added, out_ref = refs
+def dft_kernel(rows_ref, table_ref, *refs):
+    *others, out_ref = refs
     for slot in range(out_ref.shape[0]):
         rows = rows_ref[:, slot].reshape(table_ref.shape[0], rows_ref.shape[3])
         values = lax.dot_general(
             rows, table_ref[...], (((0,), (0,)), ((), ())), preferred_element_type=jnp.float32
         ).reshape(out_ref.shape[1:])
-        if total:
-            values = values + added[0][slot]
+        if others:
+            values = values + others[0][slot]
         out_ref[slot] = values.astype(out_ref.dtype)
 
 
-def dft_rows(rows, table, begin, *added, step=4):
+def dft_rows(rows, table, begin, total, first, step, *others):
     sources, slots, depth, columns = rows.shape
     depth = depth * sources
-    total = bool(added)
     out_block = (step, 2, columns // 2, table.shape[1])
-    out_spec = pl.BlockSpec(out_block, lambda block: (block, 0, 0, 0))
+    out_spec = pl.BlockSpec(out_block, lambda block: (first // step + block, 0, 0, 0))
     return pl.pallas_call(
-        functools.partial(dft_kernel, total=total),
+        dft_kernel,
         out_shape=jax.ShapeDtypeStruct(
-            (slots,) + out_block[1:], jnp.bfloat16 if total else jnp.float32
+            (total,) + out_block[1:], jnp.bfloat16 if others else jnp.float32
         ),
         grid=(pl.cdiv(slots, step),),
         in_specs=[
@@ -170,15 +179,16 @@
                 pipeline_mode=pl.Buffered(1),
             ),
         ]
-        + [out_spec] * len(added),
+        + [out_spec, pl.BlockSpec(memory_space=pl.ANY)][: len(others)],
         out_specs=out_spec,
+        input_output_aliases={3: 0} if len(others) > 1 else {},
         compiler_params=pltpu.CompilerParams(vmem_limit_bytes=58 << 20),
         cost_estimate=pl.CostEstimate(
             flops=2 * slots * columns * depth * table.shape[1],
             bytes_accessed=2 * rows.size + (2 * depth + 6 * slots * columns) * table.shape[1],
             transcendentals=0,
         ),
-    )(rows, table, *added)
+    )(rows, table, *others)
 
 
 def dft_rows_plain(rows, table):
@@ -315,6 +325,22 @@
     )(*pieces, after)
 
 
+def gate_kernel(*refs):
+    pass
+
+
+def gate(value, after):
+    anywhere = pl.BlockSpec(memory_space=pl.ANY)
+    return pl.pallas_call(
+        gate_kernel,
+        out_shape=jax.ShapeDtypeStruct(value.shape, value.dtype),
+        in_specs=[anywhere, anywhere],
+        out_specs=anywhere,
+        input_output_aliases={0: 0},
+        compiler_params=pltpu.CompilerParams(vmem_limit_bytes=58 << 20),
+    )(value, after)
+
+
 def scatter_round(terms, sources, stride, members):
     index = lax.axis_index("lat") // stride % members
     axis = 1 if stride == 1 and terms.ndim == 4 else 0
@@ -341,19 +367,29 @@
     low_m = lax.dynamic_slice_in_dim(m_of_pair, device * pairs_dev, pairs_dev)
     legend_rows = jnp.transpose(legendre, (1, 0, 2))
     coef_rows = jnp.transpose(coef, (1, 0, 2))
-    if pairs_dev % GROUP == 0 and pairs_dev > GROUP and sources == 16:
+    if pairs_dev % GROUP == 0 and pairs_dev > GROUP and sources == 16 and row_of_slot.shape[0] % (sources * STEP):
         groups = pairs_dev // GROUP
         rest = pairs_dev - GROUP
-        head = functools.partial(legendre_rows, m_of_pair, row_of_slot, legend_rows, coef_rows)
-        outgoing = head(groups - 1, 1, 4)
+        head = functools.partial(legendre_rows, m_of_pair, legend_rows, coef_rows)
+        slots = row_of_slot.shape[0]
+        slots_dev = slots // sources
+        main = slots_dev - slots_dev % STEP
+        (outgoing,) = head(row_of_slot, [slots], groups - 1, 1, 4)
         first_in = exchange(outgoing, sources)
-        second_in = exchange(head(0, groups - 1, 2), sources)
+        by_device = row_of_slot.reshape(sources, slots_dev)
+        order = jnp.concatenate([by_device[:, :main].reshape(-1), by_device[:, main:].reshape(-1)])
+        main_out, last_out = head(
+            order, [sources * main, sources * (slots_dev - main)], 0, groups - 1, 2
+        )
+        main_in = exchange(main_out, sources)
         table = dft_table(m_of_pair, wave_count, pairs_dev, ((0, rest), (rest, pairs_dev)))
-        partial = dft_rows(first_in, table, 4 * sources * rest)
-        grid_out = dft_rows(second_in, table, 0, partial)
+        partial = dft_rows(first_in, table, 4 * sources * rest, slots_dev, 0, STEP)
+        grid_out = dft_rows(main_in, table, 0, slots_dev, 0, STEP, partial)
         terms = spectrum_sums(m_of_pair, coef_rows, outgoing)
         terms = terms.reshape(sources // 4, 4, -1, columns // 2)
         terms = sum_pieces(scatter_round(terms, sources, 1, 4), partial)
+        last_in = exchange(gate(last_out, terms), sources)
+        grid_out = dft_rows(last_in, table, 0, slots_dev, main, 1, partial, grid_out)
         terms = terms.reshape(sources // 4, -1, columns // 2)
         pieces = scatter_round(terms, sources, 4, sources // 4)
         spectrum = sum_pieces(pieces, grid_out, wave_count)

time: 246 us -> 245 us (level)
  waiting for transfers between devices: 106 us -> 91.1 us
  starting transfers between devices: 16.4 us -> 21.9 us
  Pallas kernels: 76.7 us -> 80.4 us
    all_to_all x2 -> x3, waiting for transfers between devices: 106 us -> 91.1 us  [exchange(): lax.all_to_all(outgoing.reshape(outgoing.shape[0], -1, outgoing.shape[3])...]
    all_to_all x2 -> x3, starting transfers between devices: 11.6 us -> 16.5 us  [exchange(): lax.all_to_all(outgoing.reshape(outgoing.shape[0], -1, outgoing.shape[3])...]
    pallas_call x2 -> x4, Pallas kernels: 28 us -> 31.8 us  [the longest x3 31.8 us: dft_rows(): pl.pallas_call(dft_kernel, out_shape=jax.ShapeDtypeStruct((total,) + out_...]
  transfers between devices with their start and end apart: 8 -> 9, of which waited for: 2 -> 3; matrix products, arithmetic and copies ran while one was open for 18% -> 19% of each run, Pallas kernels for 25% -> 27%
where the time goes in v4:
time: 245 us; the launch traced here: 242 us
  waiting for transfers between devices  91.1 us (37%)
  Pallas kernels  80.4 us (33%)
  other arithmetic  41.8 us (17%)
  starting transfers between devices  21.9 us (9%)
  local copies, waits for them, and re-layouts  6.4 us (3%)
    all_to_all x3, waiting for transfers between devices, exchange(): lax.all_to_all(outgoing.reshape(outgoing.shape[0], -1, outgoing.shape[3])...  91.1 us
    convert_element_type x1, other arithmetic, dft_table(): return (weights * jnp.cos(angles)).astype(jnp.bfloat16)  41.1 us
    pallas_call x2, Pallas kernels, legendre_rows(): pl.pallas_call(functools.partial(legendre_kernel, length=length, first=fi...  37.4 us
    pallas_call x3, Pallas kernels, dft_rows(): pl.pallas_call(dft_kernel, out_shape=jax.ShapeDtypeStruct((total,) + out_...  31.8 us
    all_to_all x3, starting transfers between devices, exchange(): lax.all_to_all(outgoing.reshape(outgoing.shape[0], -1, outgoing.shape[3])...  16.5 us
    pallas_call x1, Pallas kernels, spectrum_sums(): pl.pallas_call(functools.partial(spectrum_kernel, pairs_dev=pairs_dev), o...  8.13 us
    ppermute x6, starting transfers between devices, scatter_round(): pieces.append(lax.ppermute(mine(step), 'lat', pairs))  5.43 us
  transfers between devices with their start and end apart: 9, of which 3 were waited for; matrix products, arithmetic and copies ran while one was open for 19% of the time, Pallas kernels for 27%

profile of v4, /device:TPU:15, one launch (start us, length us, event | category | flops | bytes accessed | tf_op | source)
XLA Modules:
  0.0 242.4 jit_solution(14094764282504539399)
XLA Ops:
  0.6 14.0 %shard_map.69.after_ref = bf16[368,4,8,128]{3,2,1,0:T(8,128)(2,1)} custom-call(s32[384]{0:T(512)} %wave_ref.5, s32[368]{0:T(512)} %slot_ref.1, bf16[769,24,360]{2,1,0:T(8,128)(2,1)} %bitcast.38, bf16[769,24,128]{2,1,0:T(8,128)(2,1)} %bitcast.35), custom_call_target="tpu_custom_call" | custom-call | flops 3353149440 | bytes 9019008 | tf_op jit(solution)/shard_map/pallas_call | solution.py:97
  14.6 6.5 %all-to-all-start = ((bf16[368,32,128]{2,1,0:T(8,128)(2,1)}), bf16[368,32,128]{2,1,0:T(8,128)(2,1)S(1)}, u32[]{:S(2)}, u32[]{:S(2)}) async-start(bf16[368,32,128]{2,1,0:T(8,128)(2,1)} %bitcast.34), calls=%async_computation | async-start | bytes 6029312 | tf_op jit(solution)/shard_map/all_to_all | solution.py:356
  21.5 0.7 pad_add_fusion.1.slot_ref
  22.1 23.5 %shard_map.68 = (bf16[320,4,16,128]{3,2,1,0:T(8,128)(2,1)}, bf16[48,4,16,128]{3,2,1,0:T(8,128)(2,1)}) custom-call(s32[384]{0:T(512)} %wave_ref.5, s32[368]{0:T(512)} %pad_add_fusion.1.slot_ref, bf16[769,24,360]{2,1,0:T(8,128)(2,1)} %bitcast.39, bf16[769,24,128]{2,1,0:T(8,128)(2,1)} %bitcast.36), custom_call_target="tpu_custom_call" | custom-call | flops 6706298880 | bytes 18038016 | tf_op jit(solution)/shard_map/pallas_call | solution.py:97
  45.6 42.6 %all-to-all-done = bf16[368,32,128]{2,1,0:T(8,128)(2,1)S(1)} async-done(((bf16[368,32,128]{2,1,0:T(8,128)(2,1)}), bf16[368,32,128]{2,1,0:T(8,128)(2,1)S(1)}, u32[]{:S(2)}, u32[]{:S(2)}) %all-to-all-start) | async-done | bytes 3014688 | tf_op jit(solution)/shard_map/all_to_all | solution.py:356
  88.2 5.0 %all-to-all-start.2 = ((bf16[320,64,128]{2,1,0:T(8,128)(2,1)}), bf16[320,64,128]{2,1,0:T(8,128)(2,1)}, u32[]{:S(2)}, u32[]{:S(2)}) async-start(bf16[320,64,128]{2,1,0:T(8,128)(2,1)} %bitcast.41), calls=%async_computation.2 | async-start | bytes 10485760 | tf_op jit(solution)/shard_map/all_to_all | solution.py:356
  93.3 8.1 %shard_map.70 = f32[768,64]{1,0:T(8,128)} custom-call(s32[384]{0:T(512)} %wave_ref.5, bf16[769,24,128]{2,1,0:T(8,128)(2,1)} %bitcast.37, bf16[368,4,8,128]{3,2,1,0:T(8,128)(2,1)} %shard_map.69.after_ref), custom_call_target="tpu_custom_call" | custom-call | flops 18898944 | bytes 4724736 | tf_op jit(solution)/shard_map/pallas_call | solution.py:280
  101.4 1.7 dynamic-slice_bitcast_fusion
  103.6 1.2 collective-permute-start.1
  106.1 41.1 %fusion.4.table_ref = bf16[1536,1440]{1,0:T(8,128)(2,1)} fusion(s32[1536]{0:T(1024)S(1)} %pad_add_fusion, s32[1536]{0:T(1024)S(1)} %constant_dynamic-update-slice_fusion, f32[1536]{0:T(1024)S(1)} %compare_select_fusion), kind=kLoop, calls=%fused_computation.5 | loop fusion | flops 26542080 | bytes 4442112 | tf_op jit(solution)/shard_map/convert_element_type | solution.py:214
  147.2 10.8 %shard_map.71.refs_3_.refs_0_ = f32[23,2,64,1440]{3,2,1,0:T(8,128)} custom-call(bf16[16,23,32,128]{3,2,1,0:T(8,128)(2,1)} %bitcast.40, bf16[1536,1440]{1,0:T(8,128)(2,1)} %fusion.4.table_ref), custom_call_target="tpu_custom_call" | custom-call | flops 4341104640 | bytes 29925376 | tf_op jit(solution)/shard_map/pallas_call | solution.py:168
  158.0 0.6 copy-done.2
  158.7 1.7 shard_map.72.refs_1_
  160.4 47.9 %all-to-all-done.2 = bf16[320,64,128]{2,1,0:T(8,128)(2,1)} async-done(((bf16[320,64,128]{2,1,0:T(8,128)(2,1)}), bf16[320,64,128]{2,1,0:T(8,128)(2,1)}, u32[]{:S(2)}, u32[]{:S(2)}) %all-to-all-start.2) | async-done | bytes 5242912 | tf_op jit(solution)/shard_map/all_to_all | solution.py:356
  208.2 4.9 %all-to-all-start.1 = ((bf16[48,64,128]{2,1,0:T(8,128)(2,1)}), bf16[48,64,128]{2,1,0:T(8,128)(2,1)S(1)}, u32[]{:S(2)}, u32[]{:S(2)}) async-start(bf16[48,64,128]{2,1,0:T(8,128)(2,1)} %bitcast.42), calls=%async_computation.1 | async-start | bytes 1572864 | tf_op jit(solution)/shard_map/all_to_all | solution.py:356
  213.2 1.4 dynamic-slice_bitcast_fusion.3
  214.6 1.2 collective-permute-start.5
  215.7 1.2 collective-permute-start.4
  216.9 0.9 collective-permute-start.3
  217.8 15.5 %shard_map.74.refs_1_ = bf16[23,2,64,1440]{3,2,1,0:T(8,128)(2,1)} custom-call(bf16[16,20,64,128]{3,2,1,0:T(8,128)(2,1)} %bitcast.16.rows_ref, bf16[1536,1440]{1,0:T(8,128)(2,1)} %fusion.4.table_ref, f32[23,2,64,1440]{3,2,1,0:T(8,128)} %shard_map.71.refs_3_.refs_0_), custom_call_target="tpu_custom_call" | custom-call | flops 7549747200 | bytes 30310400 | tf_op jit(solution)/shard_map/pallas_call | solution.py:168
  233.3 0.6 all-to-all-done.1
  233.9 0.9 copy-done.1
  234.8 5.6 %shard_map.75.refs_3_ = bf16[23,2,64,1440]{3,2,1,0:T(8,128)(2,1)} custom-call(bf16[16,3,64,128]{3,2,1,0:T(8,128)(2,1)} %bitcast.43, bf16[1536,1440]{1,0:T(8,128)(2,1)} %fusion.4.table_ref, f32[23,2,64,1440]{3,2,1,0:T(8,128)} %shard_map.71.refs_3_.refs_0_, bf16[23,2,64,1440]{3,2,1,0:T(8,128)(2,1)} %shard_map.74.refs_1_), custom_call_target="tpu_custom_call", output_to_operand_aliasing={{}: (3, {})} | custom-call | flops 1132462080 | bytes 7053312 | tf_op jit(solution)/shard_map/pallas_call | solution.py:168
  241.0 1.4 shard_map.76
  (48 shorter events, 2.9 us)
Async XLA Ops:
  0.6 20.5 %copy-start.9 = (s32[368]{0:T(512)S(1)}, s32[368]{0:T(512)}, u32[]{:S(2)}) copy-start(s32[368]{0:T(512)} %slot_ref.1) | copy-start | bytes 4420
  14.6 73.6 %all-to-all-start = ((bf16[368,32,128]{2,1,0:T(8,128)(2,1)}), bf16[368,32,128]{2,1,0:T(8,128)(2,1)S(1)}, u32[]{:S(2)}, u32[]{:S(2)}) async-start(bf16[368,32,128]{2,1,0:T(8,128)(2,1)} %bitcast.34), calls=%async_computation | async-start | bytes 6029312 | tf_op jit(solution)/shard_map/all_to_all | solution.py:356
  88.2 14.9 %copy-start = (bf16[368,32,128]{2,1,0:T(8,128)(2,1)}, bf16[368,32,128]{2,1,0:T(8,128)(2,1)S(1)}, u32[]{:S(2)}) copy-start(bf16[368,32,128]{2,1,0:T(8,128)(2,1)S(1)} %all-to-all-done) | copy-start | bytes 9043972
  88.2 17.0 %copy-start.8 = (s32[384]{0:T(512)S(1)}, s32[384]{0:T(512)}, u32[]{:S(2)}) copy-start(s32[384]{0:T(512)} %wave_ref.5) | copy-start | bytes 4612
  88.2 120.0 %all-to-all-start.2 = ((bf16[320,64,128]{2,1,0:T(8,128)(2,1)}), bf16[320,64,128]{2,1,0:T(8,128)(2,1)}, u32[]{:S(2)}, u32[]{:S(2)}) async-start(bf16[320,64,128]{2,1,0:T(8,128)(2,1)} %bitcast.41), calls=%async_computation.2 | async-start | bytes 10485760 | tf_op jit(solution)/shard_map/all_to_all | solution.py:356
  103.1 54.8 %collective-permute-start.2 = (f32[4,48,64]{2,1,0:T(8,128)S(1)}, f32[4,48,64]{2,1,0:T(8,128)S(1)}, u32[]{:S(2)}, u32[]{:S(2)}) collective-permute-start(f32[4,48,64]{2,1,0:T(8,128)S(1)} %get-tuple-element.6), channel_id=1, source_target_pairs={{0,3},{1,2},{2,1},{3,0},{4,7},{5,6},{6,5},{7,4},{8,11},{9,10},{10,... | collective-permute-start | bytes 147464 | tf_op jit(solution)/shard_map/ppermute | solution.py:351
  103.6 54.3 %collective-permute-start.1 = (f32[4,48,64]{2,1,0:T(8,128)S(1)}, f32[4,48,64]{2,1,0:T(8,128)S(1)}, u32[]{:S(2)}, u32[]{:S(2)}) collective-permute-start(f32[4,48,64]{2,1,0:T(8,128)S(1)} %get-tuple-element.7), channel_id=1, source_target_pairs={{0,2},{1,3},{2,0},{3,1},{4,6},{5,7},{6,4},{7,5},{8,10},{9,11},{10,... | collective-permute-start | bytes 147464 | tf_op jit(solution)/shard_map/ppermute | solution.py:351
  104.8 53.2 %collective-permute-start = (f32[4,48,64]{2,1,0:T(8,128)S(1)}, f32[4,48,64]{2,1,0:T(8,128)S(1)}, u32[]{:S(2)}, u32[]{:S(2)}) collective-permute-start(f32[4,48,64]{2,1,0:T(8,128)S(1)} %get-tuple-element.8), channel_id=1, source_target_pairs={{0,1},{1,0},{2,3},{3,2},{4,5},{5,4},{6,7},{7,6},{8,9},{9,8},{10,11... | collective-permute-start | bytes 147464 | tf_op jit(solution)/shard_map/ppermute | solution.py:351
  158.0 0.6 copy-start.2
  158.0 0.7 copy-start.3
  158.0 0.7 copy-start.4
  208.2 25.7 %all-to-all-start.1 = ((bf16[48,64,128]{2,1,0:T(8,128)(2,1)}), bf16[48,64,128]{2,1,0:T(8,128)(2,1)S(1)}, u32[]{:S(2)}, u32[]{:S(2)}) async-start(bf16[48,64,128]{2,1,0:T(8,128)(2,1)} %bitcast.42), calls=%async_computation.1 | async-start | bytes 1572864 | tf_op jit(solution)/shard_map/all_to_all | solution.py:356
  214.6 25.8 %collective-permute-start.5 = (f32[48,64]{1,0:T(8,128)S(1)}, f32[48,64]{1,0:T(8,128)S(1)}, u32[]{:S(2)}, u32[]{:S(2)}) collective-permute-start(f32[48,64]{1,0:T(8,128)S(1)} %get-tuple-element.10), channel_id=1, source_target_pairs={{0,12},{1,13},{2,14},{3,15},{4,8},{5,9},{6,10},{7,11},{8,4},{9,5},... | collective-permute-start | bytes 36872 | tf_op jit(solution)/shard_map/ppermute | solution.py:351
  215.7 24.6 %collective-permute-start.4 = (f32[48,64]{1,0:T(8,128)S(1)}, f32[48,64]{1,0:T(8,128)S(1)}, u32[]{:S(2)}, u32[]{:S(2)}) collective-permute-start(f32[48,64]{1,0:T(8,128)S(1)} %get-tuple-element.11), channel_id=1, source_target_pairs={{0,8},{1,9},{2,10},{3,11},{4,12},{5,13},{6,14},{7,15},{8,0},{9,1},... | collective-permute-start | bytes 36872 | tf_op jit(solution)/shard_map/ppermute | solution.py:351
  216.9 23.5 %collective-permute-start.3 = (f32[48,64]{1,0:T(8,128)S(1)}, f32[48,64]{1,0:T(8,128)S(1)}, u32[]{:S(2)}, u32[]{:S(2)}) collective-permute-start(f32[48,64]{1,0:T(8,128)S(1)} %get-tuple-element.12), channel_id=1, source_target_pairs={{0,4},{1,5},{2,6},{3,7},{4,0},{5,1},{6,2},{7,3},{8,12},{9,13},{10,... | collective-permute-start | bytes 36872 | tf_op jit(solution)/shard_map/ppermute | solution.py:351
  233.9 0.9 copy-start.1
  240.3 0.6 copy-start.5
  240.4 0.6 copy-start.6
  240.4 0.6 copy-start.7

commit v5 on v4

--- a/solution.py
+++ b/solution.py
@@ -10,7 +10,7 @@
 
 NLON = 1440
 GROUP = 8
-STEP = 4
+STEP = 3
 LANES = 128
 
 
@@ -374,7 +374,7 @@
         slots = row_of_slot.shape[0]
         slots_dev = slots // sources
         main = slots_dev - slots_dev % STEP
-        (outgoing,) = head(row_of_slot, [slots], groups - 1, 1, 4)
+        (outgoing,) = head(row_of_slot, [slots], groups - 1, 1, 8)
         first_in = exchange(outgoing, sources)
         by_device = row_of_slot.reshape(sources, slots_dev)
         order = jnp.concatenate([by_device[:, :main].reshape(-1), by_device[:, main:].reshape(-1)])
@@ -388,10 +388,10 @@
         terms = spectrum_sums(m_of_pair, coef_rows, outgoing)
         terms = terms.reshape(sources // 4, 4, -1, columns // 2)
         terms = sum_pieces(scatter_round(terms, sources, 1, 4), partial)
-        last_in = exchange(gate(last_out, terms), sources)
-        grid_out = dft_rows(last_in, table, 0, slots_dev, main, 1, partial, grid_out)
         terms = terms.reshape(sources // 4, -1, columns // 2)
         pieces = scatter_round(terms, sources, 4, sources // 4)
+        last_in = exchange(gate(last_out, pieces[0]), sources)
+        grid_out = dft_rows(last_in, table, 0, slots_dev, main, 1, partial, grid_out)
         spectrum = sum_pieces(pieces, grid_out, wave_count)
     else:
         outgoing = legendre_rows_plain(low_m, row_of_slot, legend_rows, coef_rows)

time: 245 us -> 249 us (1.016)
  waiting for transfers between devices: 91.1 us -> 93.8 us
    all_to_all x3, waiting for transfers between devices: 91.1 us -> 93.8 us  [exchange(): lax.all_to_all(outgoing.reshape(outgoing.shape[0], -1, outgoing.shape[3])...]
  transfers between devices with their start and end apart: 9 -> 9, of which waited for: 3 -> 2; matrix products, arithmetic and copies ran while one was open for 19% -> 19% of each run, Pallas kernels for 27% -> 27%
where the time goes in v5:
time: 249 us; the launch traced here: 246 us
  waiting for transfers between devices  93.8 us (38%)
  Pallas kernels  80.6 us (32%)
  other arithmetic  41.8 us (17%)
  starting transfers between devices  21.9 us (9%)
  local copies, waits for them, and re-layouts  6.92 us (3%)
    all_to_all x3, waiting for transfers between devices, exchange(): lax.all_to_all(outgoing.reshape(outgoing.shape[0], -1, outgoing.shape[3])...  93.8 us
    convert_element_type x1, other arithmetic, dft_table(): return (weights * jnp.cos(angles)).astype(jnp.bfloat16)  41.1 us
    pallas_call x2, Pallas kernels, legendre_rows(): pl.pallas_call(functools.partial(legendre_kernel, length=length, first=fi...  36.9 us
    pallas_call x3, Pallas kernels, dft_rows(): pl.pallas_call(dft_kernel, out_shape=jax.ShapeDtypeStruct((total,) + out_...  32.5 us
    all_to_all x3, starting transfers between devices, exchange(): lax.all_to_all(outgoing.reshape(outgoing.shape[0], -1, outgoing.shape[3])...  16.5 us
    pallas_call x1, Pallas kernels, spectrum_sums(): pl.pallas_call(functools.partial(spectrum_kernel, pairs_dev=pairs_dev), o...  8.14 us
    ppermute x6, starting transfers between devices, scatter_round(): pieces.append(lax.ppermute(mine(step), 'lat', pairs))  5.43 us
  transfers between devices with their start and end apart: 9, of which 2 were waited for; matrix products, arithmetic and copies ran while one was open for 19% of the time, Pallas kernels for 27%

profile of v5, /device:TPU:15, one launch (start us, length us, event | category | flops | bytes accessed | tf_op | source)
XLA Modules:
  0.0 245.9 jit_solution(193197755621889386)
XLA Ops:
  0.6 13.4 %shard_map.69.after_ref = bf16[368,4,8,128]{3,2,1,0:T(8,128)(2,1)} custom-call(s32[384]{0:T(512)} %wave_ref.5, s32[368]{0:T(512)} %slot_ref.1, bf16[769,24,360]{2,1,0:T(8,128)(2,1)} %bitcast.38, bf16[769,24,128]{2,1,0:T(8,128)(2,1)} %bitcast.35), custom_call_target="tpu_custom_call" | custom-call | flops 3353149440 | bytes 9019008 | tf_op jit(solution)/shard_map/pallas_call | solution.py:97
  14.0 6.5 %all-to-all-start = ((bf16[368,32,128]{2,1,0:T(8,128)(2,1)}), bf16[368,32,128]{2,1,0:T(8,128)(2,1)S(1)}, u32[]{:S(2)}, u32[]{:S(2)}) async-start(bf16[368,32,128]{2,1,0:T(8,128)(2,1)} %bitcast.34), calls=%async_computation | async-start | bytes 6029312 | tf_op jit(solution)/shard_map/all_to_all | solution.py:356
  20.9 0.7 pad_add_fusion.1.slot_ref
  21.6 23.5 %shard_map.68 = (bf16[336,4,16,128]{3,2,1,0:T(8,128)(2,1)}, bf16[32,4,16,128]{3,2,1,0:T(8,128)(2,1)}) custom-call(s32[384]{0:T(512)} %wave_ref.5, s32[368]{0:T(512)} %pad_add_fusion.1.slot_ref, bf16[769,24,360]{2,1,0:T(8,128)(2,1)} %bitcast.39, bf16[769,24,128]{2,1,0:T(8,128)(2,1)} %bitcast.36), custom_call_target="tpu_custom_call" | custom-call | flops 6706298880 | bytes 18038016 | tf_op jit(solution)/shard_map/pallas_call | solution.py:97
  45.1 42.6 %all-to-all-done = bf16[368,32,128]{2,1,0:T(8,128)(2,1)S(1)} async-done(((bf16[368,32,128]{2,1,0:T(8,128)(2,1)}), bf16[368,32,128]{2,1,0:T(8,128)(2,1)S(1)}, u32[]{:S(2)}, u32[]{:S(2)}) %all-to-all-start) | async-done | bytes 3014688 | tf_op jit(solution)/shard_map/all_to_all | solution.py:356
  87.6 5.0 %all-to-all-start.2 = ((bf16[336,64,128]{2,1,0:T(8,128)(2,1)}), bf16[336,64,128]{2,1,0:T(8,128)(2,1)}, u32[]{:S(2)}, u32[]{:S(2)}) async-start(bf16[336,64,128]{2,1,0:T(8,128)(2,1)} %bitcast.41), calls=%async_computation.2 | async-start | bytes 11010048 | tf_op jit(solution)/shard_map/all_to_all | solution.py:356
  92.7 8.1 %shard_map.70 = f32[768,64]{1,0:T(8,128)} custom-call(s32[384]{0:T(512)} %wave_ref.5, bf16[769,24,128]{2,1,0:T(8,128)(2,1)} %bitcast.37, bf16[368,4,8,128]{3,2,1,0:T(8,128)(2,1)} %shard_map.69.after_ref), custom_call_target="tpu_custom_call" | custom-call | flops 18898944 | bytes 4724736 | tf_op jit(solution)/shard_map/pallas_call | solution.py:280
  100.8 1.7 dynamic-slice_bitcast_fusion
  103.0 1.2 collective-permute-start.1
  105.6 41.1 %fusion.4.table_ref = bf16[1536,1440]{1,0:T(8,128)(2,1)} fusion(s32[1536]{0:T(1024)S(1)} %pad_add_fusion, s32[1536]{0:T(1024)S(1)} %constant_dynamic-update-slice_fusion, f32[1536]{0:T(1024)S(1)} %compare_select_fusion), kind=kLoop, calls=%fused_computation.5 | loop fusion | flops 26542080 | bytes 4442112 | tf_op jit(solution)/shard_map/convert_element_type | solution.py:214
  146.6 11.6 %shard_map.71.refs_3_.refs_0_ = f32[23,2,64,1440]{3,2,1,0:T(8,128)} custom-call(bf16[16,23,32,128]{3,2,1,0:T(8,128)(2,1)} %bitcast.40, bf16[1536,1440]{1,0:T(8,128)(2,1)} %fusion.4.table_ref), custom_call_target="tpu_custom_call" | custom-call | flops 4341104640 | bytes 29925376 | tf_op jit(solution)/shard_map/pallas_call | solution.py:168
  158.2 0.6 copy-done.2
  158.9 1.7 shard_map.72
  160.6 1.4 dynamic-slice_bitcast_fusion.3
  162.0 51.3 %all-to-all-done.2 = bf16[336,64,128]{2,1,0:T(8,128)(2,1)} async-done(((bf16[336,64,128]{2,1,0:T(8,128)(2,1)}), bf16[336,64,128]{2,1,0:T(8,128)(2,1)}, u32[]{:S(2)}, u32[]{:S(2)}) %all-to-all-start.2) | async-done | bytes 5505056 | tf_op jit(solution)/shard_map/all_to_all | solution.py:356
  213.3 4.9 %all-to-all-start.1 = ((bf16[32,64,128]{2,1,0:T(8,128)(2,1)}), bf16[32,64,128]{2,1,0:T(8,128)(2,1)S(1)}, u32[]{:S(2)}, u32[]{:S(2)}) async-start(bf16[32,64,128]{2,1,0:T(8,128)(2,1)} %bitcast.43), calls=%async_computation.1 | async-start | bytes 1048576 | tf_op jit(solution)/shard_map/all_to_all | solution.py:356
  218.2 1.2 collective-permute-start.5
  219.4 1.2 collective-permute-start.4
  220.5 0.9 collective-permute-start.3
  221.5 16.7 %shard_map.74.refs_1_ = bf16[23,2,64,1440]{3,2,1,0:T(8,128)(2,1)} custom-call(bf16[16,21,64,128]{3,2,1,0:T(8,128)(2,1)} %bitcast.18.rows_ref, bf16[1536,1440]{1,0:T(8,128)(2,1)} %fusion.4.table_ref, f32[23,2,64,1440]{3,2,1,0:T(8,128)} %shard_map.71.refs_3_.refs_0_), custom_call_target="tpu_custom_call" | custom-call | flops 7927234560 | bytes 31678464 | tf_op jit(solution)/shard_map/pallas_call | solution.py:168
  238.2 0.8 copy-done.1
  239.0 4.2 %shard_map.75.refs_3_ = bf16[23,2,64,1440]{3,2,1,0:T(8,128)(2,1)} custom-call(bf16[16,2,64,128]{3,2,1,0:T(8,128)(2,1)} %bitcast.42, bf16[1536,1440]{1,0:T(8,128)(2,1)} %fusion.4.table_ref, f32[23,2,64,1440]{3,2,1,0:T(8,128)} %shard_map.71.refs_3_.refs_0_, bf16[23,2,64,1440]{3,2,1,0:T(8,128)(2,1)} %shard_map.74.refs_1_), custom_call_target="tpu_custom_call", output_to_operand_aliasing={{}: (3, {})} | custom-call | flops 754974720 | bytes 5685248 | tf_op jit(solution)/shard_map/pallas_call | solution.py:168
  243.8 0.6 copy-done.7
  244.5 1.4 shard_map.76
  (48 shorter events, 2.8 us)
Async XLA Ops:
  0.6 19.9 %copy-start.9 = (s32[368]{0:T(512)S(1)}, s32[368]{0:T(512)}, u32[]{:S(2)}) copy-start(s32[368]{0:T(512)} %slot_ref.1) | copy-start | bytes 4420
  14.0 73.6 %all-to-all-start = ((bf16[368,32,128]{2,1,0:T(8,128)(2,1)}), bf16[368,32,128]{2,1,0:T(8,128)(2,1)S(1)}, u32[]{:S(2)}, u32[]{:S(2)}) async-start(bf16[368,32,128]{2,1,0:T(8,128)(2,1)} %bitcast.34), calls=%async_computation | async-start | bytes 6029312 | tf_op jit(solution)/shard_map/all_to_all | solution.py:356
  87.6 13.2 %copy-start = (bf16[368,32,128]{2,1,0:T(8,128)(2,1)}, bf16[368,32,128]{2,1,0:T(8,128)(2,1)S(1)}, u32[]{:S(2)}) copy-start(bf16[368,32,128]{2,1,0:T(8,128)(2,1)S(1)} %all-to-all-done) | copy-start | bytes 9043972
  87.6 17.1 %copy-start.8 = (s32[384]{0:T(512)S(1)}, s32[384]{0:T(512)}, u32[]{:S(2)}) copy-start(s32[384]{0:T(512)} %wave_ref.5) | copy-start | bytes 4612
  87.6 125.6 %all-to-all-start.2 = ((bf16[336,64,128]{2,1,0:T(8,128)(2,1)}), bf16[336,64,128]{2,1,0:T(8,128)(2,1)}, u32[]{:S(2)}, u32[]{:S(2)}) async-start(bf16[336,64,128]{2,1,0:T(8,128)(2,1)} %bitcast.41), calls=%async_computation.2 | async-start | bytes 11010048 | tf_op jit(solution)/shard_map/all_to_all | solution.py:356
  102.5 55.7 %collective-permute-start.2 = (f32[4,48,64]{2,1,0:T(8,128)S(1)}, f32[4,48,64]{2,1,0:T(8,128)S(1)}, u32[]{:S(2)}, u32[]{:S(2)}) collective-permute-start(f32[4,48,64]{2,1,0:T(8,128)S(1)} %get-tuple-element.6), channel_id=1, source_target_pairs={{0,3},{1,2},{2,1},{3,0},{4,7},{5,6},{6,5},{7,4},{8,11},{9,10},{10,... | collective-permute-start | bytes 147464 | tf_op jit(solution)/shard_map/ppermute | solution.py:351
  103.0 55.2 %collective-permute-start.1 = (f32[4,48,64]{2,1,0:T(8,128)S(1)}, f32[4,48,64]{2,1,0:T(8,128)S(1)}, u32[]{:S(2)}, u32[]{:S(2)}) collective-permute-start(f32[4,48,64]{2,1,0:T(8,128)S(1)} %get-tuple-element.7), channel_id=1, source_target_pairs={{0,2},{1,3},{2,0},{3,1},{4,6},{5,7},{6,4},{7,5},{8,10},{9,11},{10,... | collective-permute-start | bytes 147464 | tf_op jit(solution)/shard_map/ppermute | solution.py:351
  104.2 54.0 %collective-permute-start = (f32[4,48,64]{2,1,0:T(8,128)S(1)}, f32[4,48,64]{2,1,0:T(8,128)S(1)}, u32[]{:S(2)}, u32[]{:S(2)}) collective-permute-start(f32[4,48,64]{2,1,0:T(8,128)S(1)} %get-tuple-element.8), channel_id=1, source_target_pairs={{0,1},{1,0},{2,3},{3,2},{4,5},{5,4},{6,7},{7,6},{8,9},{9,8},{10,11... | collective-permute-start | bytes 147464 | tf_op jit(solution)/shard_map/ppermute | solution.py:351
  158.2 0.6 copy-start.2
  158.2 0.7 copy-start.3
  158.2 0.7 copy-start.4
  213.3 24.9 %all-to-all-start.1 = ((bf16[32,64,128]{2,1,0:T(8,128)(2,1)}), bf16[32,64,128]{2,1,0:T(8,128)(2,1)S(1)}, u32[]{:S(2)}, u32[]{:S(2)}) async-start(bf16[32,64,128]{2,1,0:T(8,128)(2,1)} %bitcast.43), calls=%async_computation.1 | async-start | bytes 1048576 | tf_op jit(solution)/shard_map/all_to_all | solution.py:356
  218.2 25.0 %collective-permute-start.5 = (f32[48,64]{1,0:T(8,128)S(1)}, f32[48,64]{1,0:T(8,128)S(1)}, u32[]{:S(2)}, u32[]{:S(2)}) collective-permute-start(f32[48,64]{1,0:T(8,128)S(1)} %get-tuple-element.10), channel_id=1, source_target_pairs={{0,12},{1,13},{2,14},{3,15},{4,8},{5,9},{6,10},{7,11},{8,4},{9,5},... | collective-permute-start | bytes 36872 | tf_op jit(solution)/shard_map/ppermute | solution.py:351
  219.4 23.9 %collective-permute-start.4 = (f32[48,64]{1,0:T(8,128)S(1)}, f32[48,64]{1,0:T(8,128)S(1)}, u32[]{:S(2)}, u32[]{:S(2)}) collective-permute-start(f32[48,64]{1,0:T(8,128)S(1)} %get-tuple-element.11), channel_id=1, source_target_pairs={{0,8},{1,9},{2,10},{3,11},{4,12},{5,13},{6,14},{7,15},{8,0},{9,1},... | collective-permute-start | bytes 36872 | tf_op jit(solution)/shard_map/ppermute | solution.py:351
  220.5 22.7 %collective-permute-start.3 = (f32[48,64]{1,0:T(8,128)S(1)}, f32[48,64]{1,0:T(8,128)S(1)}, u32[]{:S(2)}, u32[]{:S(2)}) collective-permute-start(f32[48,64]{1,0:T(8,128)S(1)} %get-tuple-element.12), channel_id=1, source_target_pairs={{0,4},{1,5},{2,6},{3,7},{4,0},{5,1},{6,2},{7,3},{8,12},{9,13},{10,... | collective-permute-start | bytes 36872 | tf_op jit(solution)/shard_map/ppermute | solution.py:351
  238.2 0.8 copy-start.1
  243.2 0.6 copy-start.5
  243.2 0.6 copy-start.6
  243.8 0.6 copy-start.7

commit v6 on v5

--- a/solution.py
+++ b/solution.py
@@ -10,7 +10,7 @@
 
 NLON = 1440
 GROUP = 8
-STEP = 3
+STEP = 4
 LANES = 128
 
 

time: 249 us -> 243 us (0.976); the launches traced: 246 us -> 242 us
  waiting for transfers between devices: 93.8 us -> 91.1 us
    all_to_all x3, waiting for transfers between devices: 93.8 us -> 91.1 us  [exchange(): lax.all_to_all(outgoing.reshape(outgoing.shape[0], -1, outgoing.shape[3])...]
  transfers between devices with their start and end apart: 9 -> 9, of which waited for: 2 -> 3; matrix products, arithmetic and copies ran while one was open for 19% -> 19% of each run, Pallas kernels for 27% -> 27%
where the time goes in v6:
time: 243 us; the launch traced here: 242 us
  waiting for transfers between devices  91.1 us (37%)
  Pallas kernels  79.9 us (33%)
  other arithmetic  41.8 us (17%)
  starting transfers between devices  21.9 us (9%)
  local copies, waits for them, and re-layouts  7 us (3%)
    all_to_all x3, waiting for transfers between devices, exchange(): lax.all_to_all(outgoing.reshape(outgoing.shape[0], -1, outgoing.shape[3])...  91.1 us
    convert_element_type x1, other arithmetic, dft_table(): return (weights * jnp.cos(angles)).astype(jnp.bfloat16)  41.1 us
    pallas_call x2, Pallas kernels, legendre_rows(): pl.pallas_call(functools.partial(legendre_kernel, length=length, first=fi...  36.8 us
    pallas_call x3, Pallas kernels, dft_rows(): pl.pallas_call(dft_kernel, out_shape=jax.ShapeDtypeStruct((total,) + out_...  31.8 us
    all_to_all x3, starting transfers between devices, exchange(): lax.all_to_all(outgoing.reshape(outgoing.shape[0], -1, outgoing.shape[3])...  16.5 us
    pallas_call x1, Pallas kernels, spectrum_sums(): pl.pallas_call(functools.partial(spectrum_kernel, pairs_dev=pairs_dev), o...  8.13 us
    ppermute x6, starting transfers between devices, scatter_round(): pieces.append(lax.ppermute(mine(step), 'lat', pairs))  5.43 us
  transfers between devices with their start and end apart: 9, of which 3 were waited for; matrix products, arithmetic and copies ran while one was open for 19% of the time, Pallas kernels for 27%

profile of v6, /device:TPU:15, one launch (start us, length us, event | category | flops | bytes accessed | tf_op | source)
XLA Modules:
  0.0 242.4 jit_solution(12991813865940075233)
XLA Ops:
  0.6 13.4 %shard_map.69.after_ref = bf16[368,4,8,128]{3,2,1,0:T(8,128)(2,1)} custom-call(s32[384]{0:T(512)} %wave_ref.5, s32[368]{0:T(512)} %slot_ref.1, bf16[769,24,360]{2,1,0:T(8,128)(2,1)} %bitcast.38, bf16[769,24,128]{2,1,0:T(8,128)(2,1)} %bitcast.35), custom_call_target="tpu_custom_call" | custom-call | flops 3353149440 | bytes 9019008 | tf_op jit(solution)/shard_map/pallas_call | solution.py:97
  14.0 6.5 %all-to-all-start = ((bf16[368,32,128]{2,1,0:T(8,128)(2,1)}), bf16[368,32,128]{2,1,0:T(8,128)(2,1)S(1)}, u32[]{:S(2)}, u32[]{:S(2)}) async-start(bf16[368,32,128]{2,1,0:T(8,128)(2,1)} %bitcast.34), calls=%async_computation | async-start | bytes 6029312 | tf_op jit(solution)/shard_map/all_to_all | solution.py:356
  20.9 0.7 pad_add_fusion.1.slot_ref
  21.6 23.5 %shard_map.68 = (bf16[320,4,16,128]{3,2,1,0:T(8,128)(2,1)}, bf16[48,4,16,128]{3,2,1,0:T(8,128)(2,1)}) custom-call(s32[384]{0:T(512)} %wave_ref.5, s32[368]{0:T(512)} %pad_add_fusion.1.slot_ref, bf16[769,24,360]{2,1,0:T(8,128)(2,1)} %bitcast.39, bf16[769,24,128]{2,1,0:T(8,128)(2,1)} %bitcast.36), custom_call_target="tpu_custom_call" | custom-call | flops 6706298880 | bytes 18038016 | tf_op jit(solution)/shard_map/pallas_call | solution.py:97
  45.0 42.6 %all-to-all-done = bf16[368,32,128]{2,1,0:T(8,128)(2,1)S(1)} async-done(((bf16[368,32,128]{2,1,0:T(8,128)(2,1)}), bf16[368,32,128]{2,1,0:T(8,128)(2,1)S(1)}, u32[]{:S(2)}, u32[]{:S(2)}) %all-to-all-start) | async-done | bytes 3014688 | tf_op jit(solution)/shard_map/all_to_all | solution.py:356
  87.6 5.0 %all-to-all-start.2 = ((bf16[320,64,128]{2,1,0:T(8,128)(2,1)}), bf16[320,64,128]{2,1,0:T(8,128)(2,1)}, u32[]{:S(2)}, u32[]{:S(2)}) async-start(bf16[320,64,128]{2,1,0:T(8,128)(2,1)} %bitcast.41), calls=%async_computation.2 | async-start | bytes 10485760 | tf_op jit(solution)/shard_map/all_to_all | solution.py:356
  92.7 8.1 %shard_map.70 = f32[768,64]{1,0:T(8,128)} custom-call(s32[384]{0:T(512)} %wave_ref.5, bf16[769,24,128]{2,1,0:T(8,128)(2,1)} %bitcast.37, bf16[368,4,8,128]{3,2,1,0:T(8,128)(2,1)} %shard_map.69.after_ref), custom_call_target="tpu_custom_call" | custom-call | flops 18898944 | bytes 4724736 | tf_op jit(solution)/shard_map/pallas_call | solution.py:280
  100.8 1.7 dynamic-slice_bitcast_fusion
  103.0 1.2 collective-permute-start.1
  105.5 41.1 %fusion.4.table_ref = bf16[1536,1440]{1,0:T(8,128)(2,1)} fusion(s32[1536]{0:T(1024)S(1)} %pad_add_fusion, s32[1536]{0:T(1024)S(1)} %constant_dynamic-update-slice_fusion, f32[1536]{0:T(1024)S(1)} %compare_select_fusion), kind=kLoop, calls=%fused_computation.5 | loop fusion | flops 26542080 | bytes 4442112 | tf_op jit(solution)/shard_map/convert_element_type | solution.py:214
  146.6 10.8 %shard_map.71.refs_3_.refs_0_ = f32[23,2,64,1440]{3,2,1,0:T(8,128)} custom-call(bf16[16,23,32,128]{3,2,1,0:T(8,128)(2,1)} %bitcast.40, bf16[1536,1440]{1,0:T(8,128)(2,1)} %fusion.4.table_ref), custom_call_target="tpu_custom_call" | custom-call | flops 4341104640 | bytes 29925376 | tf_op jit(solution)/shard_map/pallas_call | solution.py:168
  158.1 1.7 shard_map.72
  159.8 1.4 dynamic-slice_bitcast_fusion.3
  161.2 46.5 %all-to-all-done.2 = bf16[320,64,128]{2,1,0:T(8,128)(2,1)} async-done(((bf16[320,64,128]{2,1,0:T(8,128)(2,1)}), bf16[320,64,128]{2,1,0:T(8,128)(2,1)}, u32[]{:S(2)}, u32[]{:S(2)}) %all-to-all-start.2) | async-done | bytes 5242912 | tf_op jit(solution)/shard_map/all_to_all | solution.py:356
  207.7 4.9 %all-to-all-start.1 = ((bf16[48,64,128]{2,1,0:T(8,128)(2,1)}), bf16[48,64,128]{2,1,0:T(8,128)(2,1)S(1)}, u32[]{:S(2)}, u32[]{:S(2)}) async-start(bf16[48,64,128]{2,1,0:T(8,128)(2,1)} %bitcast.42), calls=%async_computation.1 | async-start | bytes 1572864 | tf_op jit(solution)/shard_map/all_to_all | solution.py:356
  212.6 1.2 collective-permute-start.5
  213.8 1.2 collective-permute-start.4
  214.9 0.9 collective-permute-start.3
  215.8 15.5 %shard_map.74.refs_1_ = bf16[23,2,64,1440]{3,2,1,0:T(8,128)(2,1)} custom-call(bf16[16,20,64,128]{3,2,1,0:T(8,128)(2,1)} %bitcast.18.rows_ref, bf16[1536,1440]{1,0:T(8,128)(2,1)} %fusion.4.table_ref, f32[23,2,64,1440]{3,2,1,0:T(8,128)} %shard_map.71.refs_3_.refs_0_), custom_call_target="tpu_custom_call" | custom-call | flops 7549747200 | bytes 30310400 | tf_op jit(solution)/shard_map/pallas_call | solution.py:168
  231.3 2.0 all-to-all-done.1
  233.3 0.9 copy-done.1
  234.2 5.6 %shard_map.75.refs_3_ = bf16[23,2,64,1440]{3,2,1,0:T(8,128)(2,1)} custom-call(bf16[16,3,64,128]{3,2,1,0:T(8,128)(2,1)} %bitcast.43, bf16[1536,1440]{1,0:T(8,128)(2,1)} %fusion.4.table_ref, f32[23,2,64,1440]{3,2,1,0:T(8,128)} %shard_map.71.refs_3_.refs_0_, bf16[23,2,64,1440]{3,2,1,0:T(8,128)(2,1)} %shard_map.74.refs_1_), custom_call_target="tpu_custom_call", output_to_operand_aliasing={{}: (3, {})} | custom-call | flops 1132462080 | bytes 7053312 | tf_op jit(solution)/shard_map/pallas_call | solution.py:168
  240.4 0.6 copy-done.7
  241.0 1.4 shard_map.76
  (48 shorter events, 3.4 us)
Async XLA Ops:
  0.6 19.9 %copy-start.9 = (s32[368]{0:T(512)S(1)}, s32[368]{0:T(512)}, u32[]{:S(2)}) copy-start(s32[368]{0:T(512)} %slot_ref.1) | copy-start | bytes 4420
  14.0 73.6 %all-to-all-start = ((bf16[368,32,128]{2,1,0:T(8,128)(2,1)}), bf16[368,32,128]{2,1,0:T(8,128)(2,1)S(1)}, u32[]{:S(2)}, u32[]{:S(2)}) async-start(bf16[368,32,128]{2,1,0:T(8,128)(2,1)} %bitcast.34), calls=%async_computation | async-start | bytes 6029312 | tf_op jit(solution)/shard_map/all_to_all | solution.py:356
  87.6 14.9 %copy-start = (bf16[368,32,128]{2,1,0:T(8,128)(2,1)}, bf16[368,32,128]{2,1,0:T(8,128)(2,1)S(1)}, u32[]{:S(2)}) copy-start(bf16[368,32,128]{2,1,0:T(8,128)(2,1)S(1)} %all-to-all-done) | copy-start | bytes 9043972
  87.6 17.0 %copy-start.8 = (s32[384]{0:T(512)S(1)}, s32[384]{0:T(512)}, u32[]{:S(2)}) copy-start(s32[384]{0:T(512)} %wave_ref.5) | copy-start | bytes 4612
  87.6 120.0 %all-to-all-start.2 = ((bf16[320,64,128]{2,1,0:T(8,128)(2,1)}), bf16[320,64,128]{2,1,0:T(8,128)(2,1)}, u32[]{:S(2)}, u32[]{:S(2)}) async-start(bf16[320,64,128]{2,1,0:T(8,128)(2,1)} %bitcast.41), calls=%async_computation.2 | async-start | bytes 10485760 | tf_op jit(solution)/shard_map/all_to_all | solution.py:356
  102.5 54.9 %collective-permute-start.2 = (f32[4,48,64]{2,1,0:T(8,128)S(1)}, f32[4,48,64]{2,1,0:T(8,128)S(1)}, u32[]{:S(2)}, u32[]{:S(2)}) collective-permute-start(f32[4,48,64]{2,1,0:T(8,128)S(1)} %get-tuple-element.6), channel_id=1, source_target_pairs={{0,3},{1,2},{2,1},{3,0},{4,7},{5,6},{6,5},{7,4},{8,11},{9,10},{10,... | collective-permute-start | bytes 147464 | tf_op jit(solution)/shard_map/ppermute | solution.py:351
  103.0 54.3 %collective-permute-start.1 = (f32[4,48,64]{2,1,0:T(8,128)S(1)}, f32[4,48,64]{2,1,0:T(8,128)S(1)}, u32[]{:S(2)}, u32[]{:S(2)}) collective-permute-start(f32[4,48,64]{2,1,0:T(8,128)S(1)} %get-tuple-element.7), channel_id=1, source_target_pairs={{0,2},{1,3},{2,0},{3,1},{4,6},{5,7},{6,4},{7,5},{8,10},{9,11},{10,... | collective-permute-start | bytes 147464 | tf_op jit(solution)/shard_map/ppermute | solution.py:351
  104.2 53.2 %collective-permute-start = (f32[4,48,64]{2,1,0:T(8,128)S(1)}, f32[4,48,64]{2,1,0:T(8,128)S(1)}, u32[]{:S(2)}, u32[]{:S(2)}) collective-permute-start(f32[4,48,64]{2,1,0:T(8,128)S(1)} %get-tuple-element.8), channel_id=1, source_target_pairs={{0,1},{1,0},{2,3},{3,2},{4,5},{5,4},{6,7},{7,6},{8,9},{9,8},{10,11... | collective-permute-start | bytes 147464 | tf_op jit(solution)/shard_map/ppermute | solution.py:351
  157.4 0.6 copy-start.2
  157.4 0.7 copy-start.3
  157.4 0.7 copy-start.4
  207.7 25.7 %all-to-all-start.1 = ((bf16[48,64,128]{2,1,0:T(8,128)(2,1)}), bf16[48,64,128]{2,1,0:T(8,128)(2,1)S(1)}, u32[]{:S(2)}, u32[]{:S(2)}) async-start(bf16[48,64,128]{2,1,0:T(8,128)(2,1)} %bitcast.42), calls=%async_computation.1 | async-start | bytes 1572864 | tf_op jit(solution)/shard_map/all_to_all | solution.py:356
  212.6 27.2 %collective-permute-start.5 = (f32[48,64]{1,0:T(8,128)S(1)}, f32[48,64]{1,0:T(8,128)S(1)}, u32[]{:S(2)}, u32[]{:S(2)}) collective-permute-start(f32[48,64]{1,0:T(8,128)S(1)} %get-tuple-element.10), channel_id=1, source_target_pairs={{0,12},{1,13},{2,14},{3,15},{4,8},{5,9},{6,10},{7,11},{8,4},{9,5},... | collective-permute-start | bytes 36872 | tf_op jit(solution)/shard_map/ppermute | solution.py:351
  213.8 26.0 %collective-permute-start.4 = (f32[48,64]{1,0:T(8,128)S(1)}, f32[48,64]{1,0:T(8,128)S(1)}, u32[]{:S(2)}, u32[]{:S(2)}) collective-permute-start(f32[48,64]{1,0:T(8,128)S(1)} %get-tuple-element.11), channel_id=1, source_target_pairs={{0,8},{1,9},{2,10},{3,11},{4,12},{5,13},{6,14},{7,15},{8,0},{9,1},... | collective-permute-start | bytes 36872 | tf_op jit(solution)/shard_map/ppermute | solution.py:351
  214.9 24.9 %collective-permute-start.3 = (f32[48,64]{1,0:T(8,128)S(1)}, f32[48,64]{1,0:T(8,128)S(1)}, u32[]{:S(2)}, u32[]{:S(2)}) collective-permute-start(f32[48,64]{1,0:T(8,128)S(1)} %get-tuple-element.12), channel_id=1, source_target_pairs={{0,4},{1,5},{2,6},{3,7},{4,0},{5,1},{6,2},{7,3},{8,12},{9,13},{10,... | collective-permute-start | bytes 36872 | tf_op jit(solution)/shard_map/ppermute | solution.py:351
  233.3 0.9 copy-start.1
  239.8 0.6 copy-start.5
  239.8 0.6 copy-start.6
  240.4 0.6 copy-start.7
